TPU v7x, 512 devices: a whole 4x4x16 slice. The times are simulated.
512 devices in a mesh: dp: 4 (over x), expert: 64 (over z, y), half: 2 (over core).
Axes of the slice: x: 4, y: 4, z: 16, core: 2. Of those that a mesh axis runs over, the one named last changes fastest.
Arguments:
- activations: bfloat16 [2, 4096, 2048], P(None, ('dp', 'expert', 'half')), parts along dimension 1, may hold values from -6 to 6
- upstream: bfloat16 [2, 4096, 2048], P(None, ('dp', 'expert', 'half')), parts along dimension 1, may hold values from -12 to 12
- routes: int32 [2, 4096, 10], P(None, ('dp', 'expert', 'half')), parts along dimension 1, may hold values from 0 to 63, all different within a row; in each aligned block of 8 rows (0 to 7, 8 to 15, ..., all dimensions but the last counted through in order) at most 2 rows name the same one
- route_gates: float32 [2, 4096, 10], P(None, ('dp', 'expert', 'half')), parts along dimension 1, may hold values from 0.05 to 0.2
- gate_matrix: bfloat16 [64, 2048, 512], P('expert', None, 'half'), may hold values from -0.125 to 0.125
- up_matrix: bfloat16 [64, 2048, 512], P('expert', None, 'half'), may hold values from -3 to 3
- down_matrix: bfloat16 [64, 512, 2048], P('expert', 'half'), may hold values from -0.25 to 0.25
Outputs:
- input_cotangent: bfloat16 [2, 4096, 2048], P(None, ('dp', 'expert', 'half')), parts along dimension 1
- down_update: bfloat16 [256, 512, 2048], P(('dp', 'expert'), 'half'), parts along dimension 0
There are 4 independent parts, one for each index of `dp`. A program takes and returns all parts, laid end to end along the dimension named above; an argument that names none is the same for every part. Nothing has to cross between parts.
Inputs may be any that keep to these rules, and one draw needn't show every extreme that they name: `routes`: each row names 10 different experts; within the rows of one device in one microbatch (aligned blocks of 8 rows) no expert is named more than 2 times, and in some blocks one expert is named exactly 2 times.
All inputs are finite; a program needn't handle non-finite values.
Results may differ from a plain program's by a relative error of at most 0.007.
Values may be sent and summed in bfloat16 or wider, within the bound.
A program may use at most 64 MiB of HBM per device.

v0:
```python
import math

import jax
import jax.numpy as jnp
from jax import lax
from jax.sharding import PartitionSpec as P

D = 2048
FF = 512
ITERS = 2


linear_term = 3.4445
cubic_term = -4.775
quintic_term = 2.0315


def contract_last(left, right):
    return lax.dot_general(
        left, right, (((1,), (1,)), ((), ())), preferred_element_type=jnp.float32
    )


def contract_first(left, right):
    return lax.dot_general(
        left, right, (((0,), (0,)), ((), ())), preferred_element_type=jnp.float32
    )


def slot_numbers(route_flat, experts, capacity):
    onehot = (route_flat[:, None] == jnp.arange(experts, dtype=jnp.int32)[None, :]).astype(
        jnp.int32
    )
    before = jnp.cumsum(onehot, axis=0) - onehot
    position = jnp.sum(before * onehot, axis=1)
    return route_flat * capacity + position


def on_device(activations, upstream, routes, route_gates, gate_matrix, up_matrix, down_matrix):
    experts = lax.axis_size("expert")
    halves = lax.axis_size("half")
    batches, tokens_dev, top = routes.shape
    width = activations.shape[2]
    capacity = max(2, 6 * tokens_dev * top // (5 * experts))
    slots = experts * capacity
    gate_local = gate_matrix[0]
    up_local = up_matrix[0]
    down_local = down_matrix[0]
    down_grad = jnp.zeros((down_local.shape[0], width), jnp.float32)
    results = []
    for batch_index in range(batches):
        route_flat = routes[batch_index].reshape(tokens_dev * top)
        slot_ids = slot_numbers(route_flat, experts, capacity)
        select = (jnp.arange(slots, dtype=jnp.int32)[:, None] == slot_ids[None, :]).astype(
            jnp.bfloat16
        )
        select_tok = jnp.sum(select.reshape(slots, tokens_dev, top), axis=2)
        token_send = jnp.dot(
            select_tok, activations[batch_index], preferred_element_type=jnp.float32
        )
        token_send = token_send.astype(jnp.bfloat16).reshape(experts, capacity, width)
        scaled = route_gates[batch_index][:, :, None] * upstream[batch_index][:, None, :].astype(
            jnp.float32
        )
        scaled = scaled.astype(jnp.bfloat16).reshape(tokens_dev * top, width)
        scaled_send = jnp.dot(select, scaled, preferred_element_type=jnp.float32)
        scaled_send = scaled_send.astype(jnp.bfloat16).reshape(experts, capacity, width)
        doubled_tokens = jnp.broadcast_to(
            token_send[:, None], (experts, halves, capacity, width)
        ).reshape(experts * halves, capacity, width)
        doubled_scaled = jnp.broadcast_to(
            scaled_send[:, None], (experts, halves, capacity, width)
        ).reshape(experts * halves, capacity, width)
        got_tokens, got_scaled = (
            lax.all_to_all(
                doubled_tokens, ("expert", "half"), split_axis=0, concat_axis=0, tiled=True
            ),
            lax.all_to_all(
                doubled_scaled, ("expert", "half"), split_axis=0, concat_axis=0, tiled=True
            ),
        )
        rows_tokens = got_tokens.reshape(experts * halves * capacity, width)
        rows_scaled = got_scaled.reshape(experts * halves * capacity, width)
        pre_gate = jnp.dot(rows_tokens, gate_local, preferred_element_type=jnp.float32)
        pre_up = jnp.dot(rows_tokens, up_local, preferred_element_type=jnp.float32)
        sigmoid_gate = jax.nn.sigmoid(pre_gate)
        activated = pre_gate * sigmoid_gate
        hidden = (activated * pre_up).astype(jnp.bfloat16)
        hidden_grad = contract_last(rows_scaled, down_local)
        gate_grad = (
            hidden_grad * pre_up * sigmoid_gate * (1.0 + pre_gate * (1.0 - sigmoid_gate))
        ).astype(jnp.bfloat16)
        up_grad = (hidden_grad * activated).astype(jnp.bfloat16)
        partial_value = contract_last(gate_grad, gate_local) + contract_last(up_grad, up_local)
        partial_value = partial_value.reshape(experts, halves, capacity, width)
        down_grad = down_grad + contract_first(hidden, rows_scaled)
        outgoing = partial_value.astype(jnp.bfloat16).reshape(experts * halves, capacity, width)
        returned = lax.all_to_all(
            outgoing, ("expert", "half"), split_axis=0, concat_axis=0, tiled=True
        )
        summed = jnp.sum(
            returned.reshape(experts, halves, capacity, width).astype(jnp.float32), axis=1
        )
        summed = summed.astype(jnp.bfloat16).reshape(slots, width)
        cotangent = contract_first(select_tok, summed).astype(jnp.bfloat16)
        results.append(cotangent)
    squares = lax.psum(jnp.sum(down_grad * down_grad), "half")
    current = down_grad / (jnp.sqrt(squares) + 1e-07)
    for iteration in range(ITERS):
        rounded = current.astype(jnp.bfloat16)
        whole_rows = lax.all_gather(rounded, "half", axis=0, tiled=True)
        gram_rows = contract_last(rounded, whole_rows)
        gram_whole = lax.all_gather(gram_rows.astype(jnp.bfloat16), "half", axis=0, tiled=True)
        square_rows = jnp.dot(
            gram_rows.astype(jnp.bfloat16), gram_whole, preferred_element_type=jnp.float32
        )
        polynomial = (cubic_term * gram_rows + quintic_term * square_rows).astype(jnp.bfloat16)
        current = linear_term * current + jnp.dot(
            polynomial, whole_rows, preferred_element_type=jnp.float32
        )
    update = (current * math.sqrt(max(FF, D))).astype(jnp.bfloat16)
    return (jnp.stack(results), update[None])


def solution(mesh):
    placed = (
        P(None, ("dp", "expert", "half"), None),
        P(None, ("dp", "expert", "half"), None),
        P(None, ("dp", "expert", "half"), None),
        P(None, ("dp", "expert", "half"), None),
        P("expert", None, "half"),
        P("expert", None, "half"),
        P("expert", "half", None),
    )
    return jax.shard_map(
        on_device,
        mesh=mesh,
        in_specs=placed,
        out_specs=(P(None, ("dp", "expert", "half"), None), P(("dp", "expert"), "half", None)),
        check_vma=False,
    )
```

profile of v0, /device:TPU:1, one launch (start us, length us, event | category | flops | bytes accessed | tf_op | source)
XLA Modules:
  0.0 425.2 jit_solution(9987742600680893849)
XLA Ops:
  13.1 20.7 %all-to-all-start.4 = ((bf16[128,2,2048]{2,1,0:T(2,128)(2,1)}), bf16[128,2,2048]{2,1,0:T(2,128)(2,1)S(1)}, u32[]{:S(2)}, u32[]{:S(2)}) async-start(bf16[128,2,2048]{2,1,0:T(2,128)(2,1)} %bitcast.14), calls=%async_computation.4 | async-start | bytes 2097152 | tf_op jit(solution)/shard_map/all_to_all | solution.py:75
  36.7 49.1 %all-to-all-done.4 = bf16[128,2,2048]{2,1,0:T(2,128)(2,1)S(1)} async-done(((bf16[128,2,2048]{2,1,0:T(2,128)(2,1)}), bf16[128,2,2048]{2,1,0:T(2,128)(2,1)S(1)}, u32[]{:S(2)}, u32[]{:S(2)}) %all-to-all-start.4) | async-done | bytes 1048608 | tf_op jit(solution)/shard_map/all_to_all | solution.py:75
  87.5 10.0 %all-to-all-start.3 = ((bf16[128,2,2048]{2,1,0:T(2,128)(2,1)}), bf16[128,2,2048]{2,1,0:T(2,128)(2,1)S(1)}, u32[]{:S(2)}, u32[]{:S(2)}) async-start(bf16[128,2,2048]{2,1,0:T(2,128)(2,1)} %bitcast.79), calls=%async_computation.3 | async-start | bytes 2097152 | tf_op jit(solution)/shard_map/all_to_all | solution.py:78
  98.8 2.2 broadcast_in_dim.39
  101.0 48.6 %all-to-all-done.3 = bf16[128,2,2048]{2,1,0:T(2,128)(2,1)S(1)} async-done(((bf16[128,2,2048]{2,1,0:T(2,128)(2,1)}), bf16[128,2,2048]{2,1,0:T(2,128)(2,1)S(1)}, u32[]{:S(2)}, u32[]{:S(2)}) %all-to-all-start.3) | async-done | bytes 1048608 | tf_op jit(solution)/shard_map/all_to_all | solution.py:78
  149.5 3.0 broadcast_in_dim.40
  152.6 10.0 %all-to-all-start.1 = ((bf16[128,2,2048]{2,1,0:T(2,128)(2,1)}), bf16[128,2,2048]{2,1,0:T(2,128)(2,1)S(1)}, u32[]{:S(2)}, u32[]{:S(2)}) async-start(bf16[128,2,2048]{2,1,0:T(2,128)(2,1)} %bitcast.77), calls=%async_computation.1 | async-start | bytes 2097152 | tf_op jit(solution)/shard_map/all_to_all | solution.py:75
  163.7 2.2 mul.144
  165.9 2.3 convolution_convert_fusion.3
  168.2 2.2 broadcast_in_dim.18
  170.4 44.3 %all-to-all-done.1 = bf16[128,2,2048]{2,1,0:T(2,128)(2,1)S(1)} async-done(((bf16[128,2,2048]{2,1,0:T(2,128)(2,1)}), bf16[128,2,2048]{2,1,0:T(2,128)(2,1)S(1)}, u32[]{:S(2)}, u32[]{:S(2)}) %all-to-all-start.1) | async-done | bytes 1048608 | tf_op jit(solution)/shard_map/all_to_all | solution.py:75
  214.6 3.0 broadcast_in_dim.38
  217.7 10.6 %all-to-all-start = ((bf16[128,2,2048]{2,1,0:T(2,128)(2,1)}), bf16[128,2,2048]{2,1,0:T(2,128)(2,1)}, u32[]{:S(2)}, u32[]{:S(2)}) async-start(bf16[128,2,2048]{2,1,0:T(2,128)(2,1)} %bitcast.78), calls=%async_computation | async-start | bytes 2097152 | tf_op jit(solution)/shard_map/all_to_all | solution.py:78
  228.8 2.4 reshape.131
  235.5 2.6 convert_element_type.147
  238.1 42.0 %all-to-all-done = bf16[128,2,2048]{2,1,0:T(2,128)(2,1)} async-done(((bf16[128,2,2048]{2,1,0:T(2,128)(2,1)}), bf16[128,2,2048]{2,1,0:T(2,128)(2,1)}, u32[]{:S(2)}, u32[]{:S(2)}) %all-to-all-start) | async-done | bytes 1048608 | tf_op jit(solution)/shard_map/all_to_all | solution.py:78
  280.1 10.4 %all-to-all-start.5 = ((bf16[128,2,2048]{2,1,0:T(2,128)(2,1)}), bf16[128,2,2048]{2,1,0:T(2,128)(2,1)}, u32[]{:S(2)}, u32[]{:S(2)}) async-start(bf16[128,2,2048]{2,1,0:T(2,128)(2,1)} %convert_element_type.147), calls=%async_computation.5 | async-start | bytes 2097152 | tf_op jit(solution)/shard_map/all_to_all | solution.py:98
  293.3 1.7 fusion.17
  297.5 2.4 multiply_reduce_fusion
  300.0 3.7 psum.7
  304.4 2.8 fusion.29
  307.1 1.7 fusion.27
  311.4 30.8 %all-to-all-done.5 = bf16[128,2,2048]{2,1,0:T(2,128)(2,1)} async-done(((bf16[128,2,2048]{2,1,0:T(2,128)(2,1)}), bf16[128,2,2048]{2,1,0:T(2,128)(2,1)}, u32[]{:S(2)}, u32[]{:S(2)}) %all-to-all-start.5) | async-done | bytes 1048608 | tf_op jit(solution)/shard_map/all_to_all | solution.py:98
  342.2 10.0 %all-to-all-start.2 = ((bf16[128,2,2048]{2,1,0:T(2,128)(2,1)}), bf16[128,2,2048]{2,1,0:T(2,128)(2,1)S(1)}, u32[]{:S(2)}, u32[]{:S(2)}) async-start(bf16[128,2,2048]{2,1,0:T(2,128)(2,1)} %convert_element_type.135), calls=%async_computation.2 | async-start | bytes 2097152 | tf_op jit(solution)/shard_map/all_to_all | solution.py:98
  352.3 3.2 fusion.71
  355.5 2.7 all_gather.13
  358.2 5.1 %fusion.72 = (bf16[256,2048]{1,0:T(8,128)(2,1)}, f32[256,2048]{1,0:T(8,128)}) fusion(bf16[512,2048]{1,0:T(8,128)(2,1)} %all-gather.3.cloned.1.call-done, bf16[256,512]{1,0:T(8,128)(2,1)S(1)} %get-tuple-element.12, bf16[512,512]{1,0:T(8,128)(2,1)S(1)} %all_gather.13, f32[256,512]{1,0:T(8,128)} %get-tuple-element.13, f32[256,2048]{1,0:T(8,128)} %get-tuple-element.11, ...), kind=kOutput, calls=%fused_computation.110 | convolution fusion | flops 673710080 | bytes 8650756 | tf_op jit(solution)/shard_map/dot_general | solution.py:118
  363.3 3.0 bitcast_reduce_fusion
  366.5 37.8 %all-to-all-done.2 = bf16[128,2,2048]{2,1,0:T(2,128)(2,1)S(1)} async-done(((bf16[128,2,2048]{2,1,0:T(2,128)(2,1)}), bf16[128,2,2048]{2,1,0:T(2,128)(2,1)S(1)}, u32[]{:S(2)}, u32[]{:S(2)}) %all-to-all-start.2) | async-done | bytes 1048608 | tf_op jit(solution)/shard_map/all_to_all | solution.py:98
  406.9 3.6 fusion.73
  410.5 4.0 all_gather.15
  414.5 3.9 fusion.4
  (97 shorter events, 28.1 us)
Async XLA Ops:
  7.2 224.0 %copy-start = (bf16[1,2048,256]{2,1,0:T(8,128)(2,1)S(1)}, bf16[1,2048,256]{2,1,0:T(8,128)(2,1)}, u32[]{:S(2)}) copy-start(bf16[1,2048,256]{2,1,0:T(8,128)(2,1)} %param.11) | copy-start | bytes 3145732
  11.4 22.3 %copy-start.17 = (bf16[2,8,2048]{2,1,0:T(8,128)(2,1)S(1)}, bf16[2,8,2048]{2,1,0:T(8,128)(2,1)}, u32[]{:S(2)}) copy-start(bf16[2,8,2048]{2,1,0:T(8,128)(2,1)} %param.8) | copy-start | bytes 196612
  13.1 21.8 %copy-start.19 = (f32[2,8,10]{2,1,0:T(8,128)S(1)}, f32[2,8,10]{2,1,0:T(8,128)}, u32[]{:S(2)}) copy-start(f32[2,8,10]{2,1,0:T(8,128)} %param.10) | copy-start | bytes 1924
  13.1 72.8 %all-to-all-start.4 = ((bf16[128,2,2048]{2,1,0:T(2,128)(2,1)}), bf16[128,2,2048]{2,1,0:T(2,128)(2,1)S(1)}, u32[]{:S(2)}, u32[]{:S(2)}) async-start(bf16[128,2,2048]{2,1,0:T(2,128)(2,1)} %bitcast.14), calls=%async_computation.4 | async-start | bytes 2097152 | tf_op jit(solution)/shard_map/all_to_all | solution.py:75
  36.7 60.9 %copy-start.18 = (bf16[2,8,2048]{2,1,0:T(8,128)(2,1)S(1)}, bf16[2,8,2048]{2,1,0:T(8,128)(2,1)}, u32[]{:S(2)}) copy-start(bf16[2,8,2048]{2,1,0:T(8,128)(2,1)} %param.7) | copy-start | bytes 196612
  87.5 62.1 %all-to-all-start.3 = ((bf16[128,2,2048]{2,1,0:T(2,128)(2,1)}), bf16[128,2,2048]{2,1,0:T(2,128)(2,1)S(1)}, u32[]{:S(2)}, u32[]{:S(2)}) async-start(bf16[128,2,2048]{2,1,0:T(2,128)(2,1)} %bitcast.79), calls=%async_computation.3 | async-start | bytes 2097152 | tf_op jit(solution)/shard_map/all_to_all | solution.py:78
  149.5 3.0 copy-start.10
  152.6 62.1 %all-to-all-start.1 = ((bf16[128,2,2048]{2,1,0:T(2,128)(2,1)}), bf16[128,2,2048]{2,1,0:T(2,128)(2,1)S(1)}, u32[]{:S(2)}, u32[]{:S(2)}) async-start(bf16[128,2,2048]{2,1,0:T(2,128)(2,1)} %bitcast.77), calls=%async_computation.1 | async-start | bytes 2097152 | tf_op jit(solution)/shard_map/all_to_all | solution.py:75
  214.6 3.0 copy-start.8
  217.7 62.4 %all-to-all-start = ((bf16[128,2,2048]{2,1,0:T(2,128)(2,1)}), bf16[128,2,2048]{2,1,0:T(2,128)(2,1)}, u32[]{:S(2)}, u32[]{:S(2)}) async-start(bf16[128,2,2048]{2,1,0:T(2,128)(2,1)} %bitcast.78), calls=%async_computation | async-start | bytes 2097152 | tf_op jit(solution)/shard_map/all_to_all | solution.py:78
  228.8 2.8 copy-start.1
  231.1 1.2 copy-start.4
  231.1 1.6 copy-start.7
  231.6 2.4 copy-start.11
  232.8 0.7 copy-start.15
  235.5 55.1 %copy-start.9 = (bf16[128,2,2048]{2,1,0:T(2,128)(2,1)S(1)}, bf16[128,2,2048]{2,1,0:T(2,128)(2,1)}, u32[]{:S(2)}) copy-start(bf16[128,2,2048]{2,1,0:T(2,128)(2,1)} %copy-done.8) | copy-start | bytes 3145732
  280.1 62.2 %all-to-all-start.5 = ((bf16[128,2,2048]{2,1,0:T(2,128)(2,1)}), bf16[128,2,2048]{2,1,0:T(2,128)(2,1)}, u32[]{:S(2)}, u32[]{:S(2)}) async-start(bf16[128,2,2048]{2,1,0:T(2,128)(2,1)} %convert_element_type.147), calls=%async_computation.5 | async-start | bytes 2097152 | tf_op jit(solution)/shard_map/all_to_all | solution.py:98
  290.5 61.8 %all-gather.3.cloned.1.call-start = ((), (), s32[]{:S(2)}) async-start(), calls=%async_computation.6 | async-start | bytes 3145728 | tf_op jit(solution)/shard_map/all_gather | solution.py:111
  293.3 1.8 copy-start.2
  295.5 0.7 copy-start.13
  296.2 1.2 copy-start.5
  296.2 1.3 copy-start.12
  296.2 1.3 copy-start.16
  307.1 1.8 copy-start.14
  309.9 42.4 %copy-start.3 = (bf16[256,2048]{1,0:T(8,128)(2,1)S(1)}, bf16[256,2048]{1,0:T(8,128)(2,1)}, u32[]{:S(2)}) copy-start(bf16[256,2048]{1,0:T(8,128)(2,1)} %fusion.29) | copy-start | bytes 3145732
  342.2 62.1 %all-to-all-start.2 = ((bf16[128,2,2048]{2,1,0:T(2,128)(2,1)}), bf16[128,2,2048]{2,1,0:T(2,128)(2,1)S(1)}, u32[]{:S(2)}, u32[]{:S(2)}) async-start(bf16[128,2,2048]{2,1,0:T(2,128)(2,1)} %convert_element_type.135), calls=%async_computation.2 | async-start | bytes 2097152 | tf_op jit(solution)/shard_map/all_to_all | solution.py:98
  352.2 54.6 %all-gather.5.cloned.1.call-start = ((), (), s32[]{:S(2)}) async-start(), calls=%async_computation.7 | async-start | bytes 3145728 | tf_op jit(solution)/shard_map/all_gather | solution.py:111
  406.9 7.6 %copy-start.6 = (bf16[512,2048]{1,0:T(8,128)(2,1)S(1)}, bf16[512,2048]{1,0:T(8,128)(2,1)}, u32[]{:S(2)}) copy-start(bf16[512,2048]{1,0:T(8,128)(2,1)} %all-gather.5.cloned.1.call-done) | copy-start | bytes 6291460
Sparse Core Ops, SparseCore 0:
  307.3 22.6 all-gather.2
  363.4 22.8 all-gather.4
where the time goes:
time: 427 us; the launch traced here: 425 us
  waiting for transfers between devices  253 us (59%)
  starting transfers between devices  71.8 us (17%)
  matrix products  33.2 us (8%)
  local copies, waits for them, and re-layouts  32.7 us (8%)
  between operations  15.1 us (4%)
  blocking collectives  10.4 us (2%)
  other arithmetic  9.36 us (2%)
    all_to_all x2, waiting for transfers between devices, on_device(): lax.all_to_all(doubled_tokens, ('expert', 'half'), split_axis=0, concat_a...  93.4 us
    all_to_all x2, waiting for transfers between devices, on_device(): lax.all_to_all(doubled_scaled, ('expert', 'half'), split_axis=0, concat_a...  90.5 us
    all_to_all x2, waiting for transfers between devices, on_device(): lax.all_to_all(outgoing, ('expert', 'half'), split_axis=0, concat_axis=0,...  68.7 us
    all_to_all x2, starting transfers between devices, on_device(): lax.all_to_all(doubled_tokens, ('expert', 'half'), split_axis=0, concat_a...  30.7 us
    all_to_all x2, starting transfers between devices, on_device(): lax.all_to_all(doubled_scaled, ('expert', 'half'), split_axis=0, concat_a...  20.6 us
    all_to_all x2, starting transfers between devices, on_device(): lax.all_to_all(outgoing, ('expert', 'half'), split_axis=0, concat_axis=0,...  20.4 us
    dot_general x8, matrix products, contract_last(): lax.dot_general(left, right, (((1,), (1,)), ((), ())), preferred_element_...  11.9 us
    dot_general x2, matrix products, on_device(): jnp.dot(polynomial, whole_rows, preferred_element_type=jnp.float32)  9.01 us
  transfers between devices with their start and end apart: 8, of which 6 were waited for; matrix products, arithmetic and copies ran while one was open for 12% of the time, Pallas kernels for 0%

commit v1 on v0

v1 whole, which is shorter than its diff:
```python
import functools
import math

import jax
import jax.numpy as jnp
from jax import lax
from jax.experimental import pallas as pl
from jax.experimental.pallas import tpu as pltpu
from jax.sharding import PartitionSpec as P

MESH = pl.DeviceIdType.MESH
NY = 4
ITERS = 2
LINEAR, CUBIC, QUINTIC = 3.4445, -4.775, 2.0315
F32, BF16 = jnp.float32, jnp.bfloat16


def nt(a, b, **kw):
    return lax.dot_general(
        a, b, (((1,), (1,)), ((), ())), preferred_element_type=F32, **kw
    )


def iota(shape, axis):
    return lax.broadcasted_iota(jnp.int32, shape, axis)


def run_both(first, second):
    live = [first, second]
    while live:
        for gen in list(live):
            try:
                next(gen)
            except StopIteration:
                live.remove(gen)


def kernel(
    NZ, act_ref, ups_ref, routes_ref, gates_ref, gate_hbm, up_hbm, down_hbm,
    cot_ref, cur_ref,
    zbuf, gbuf, ysend, ybuf, rows_tok, rows_sc, gu, down,
    part_own, part_send, part_recv, esend, ebuf, cbuf, rsend, rrecv,
    nsend, nrecv, whole, gram_b,
    w_sem, z_ss, z_rs, g_ss, g_rs, y_ss, y_rs, f_ss, f_rs, p_ss, p_rs, e_ss, e_rs,
    r_ss, r_rs, n_ss, n_rs, x_ss, x_rs, m_ss, m_rs,
):
    K = NZ // 2
    Q = K // 2
    D = zbuf.shape[-1]
    H = down.shape[0]
    D2 = D // 2
    TN = min(512, D)
    QG = rows_tok.shape[2]
    NG = Q // QG
    ex = lax.axis_index("expert")
    me = lax.axis_index("half")
    z = ex // NY
    y = ex % NY
    z_up = {"expert": ((z + 1) % NZ) * NY + y}
    z_dn = {"expert": ((z + NZ - 1) % NZ) * NY + y}
    z_to = (z_up, z_dn)
    y_to = [None] + [{"expert": z * NY + (y + r) % NY} for r in range(1, NY)]
    partner = {"half": 1 - me}
    pending = []

    def send(src, dst, ss, rs, dev):
        c = pltpu.make_async_remote_copy(
            src_ref=src, dst_ref=dst, send_sem=ss, recv_sem=rs,
            device_id=dev, device_id_type=MESH,
        )
        c.start()
        pending.append(c)

    def arrived(dst, rs, dev):
        pltpu.make_async_remote_copy(
            src_ref=dst, dst_ref=dst, send_sem=rs, recv_sem=rs,
            device_id=dev, device_id_type=MESH,
        ).wait_recv()

    weights = [
        pltpu.make_async_copy(gate_hbm.at[0], gu.at[:, pl.ds(0, H)], w_sem.at[0]),
        pltpu.make_async_copy(up_hbm.at[0], gu.at[:, pl.ds(H, H)], w_sem.at[1]),
        pltpu.make_async_copy(down_hbm.at[0], down, w_sem.at[2]),
    ]
    for w in weights:
        w.start()

    barrier = pltpu.get_barrier_semaphore()
    peers = [z_up, z_dn, partner] + y_to[1:]
    for p in peers:
        pl.semaphore_signal(barrier, inc=1, device_id=p, device_id_type=MESH)

    lane = iota((8, 128), 1)
    sub = iota((8, 128), 0)
    for m in range(2):
        zbuf[K - 1, 0, pl.ds(m * 16, 16), :] = jnp.concatenate(
            [act_ref[m].astype(F32), ups_ref[m].astype(F32)], axis=0
        ).astype(BF16)
        route = routes_ref[m]
        gate = gates_ref[m]
        gsum = jnp.zeros((8, 128), F32)
        named = jnp.zeros((8, 128), F32)
        for k in range(route.shape[1]):
            hit = route[:, k : k + 1] == lane // 2
            gsum = gsum + jnp.where(hit, gate[:, k : k + 1], 0.0)
            named = named + jnp.where(hit, 1.0, 0.0)
        before = jnp.zeros((8, 128), F32)
        for t in range(7):
            before = before + jnp.where(sub > t, named[t : t + 1, :], 0.0)
        gbuf[K - 1, 0, pl.ds(m * 8, 8), :] = jnp.where(
            before == (lane % 2).astype(F32), gsum, 0.0
        )

    pl.semaphore_wait(barrier, len(peers))

    def hop(s, d, key):
        buf = gbuf if key == "g" else zbuf
        src = buf.at[K - 1, 0] if s == 1 else buf.at[s - 2, d]
        dst = buf.at[s - 1, d] if s < K else buf.at[K - 1, 1]
        if key == "g":
            return src, dst, g_ss.at[d, s - 1], g_rs.at[d, s - 1], z_to[d]
        rows = pl.ds(key * 16, 16)
        ss, rs = z_ss.at[d, s - 1, key], z_rs.at[d, s - 1, key]
        return src.at[rows], dst.at[rows], ss, rs, z_to[d]

    def goes(s, d, key):
        return s < K or (s == K and (d == 0 if key == "g" else key == d))

    pieces = [(d, key) for key in ("g", 0, 1) for d in range(2)]
    for d, key in pieces:
        send(*hop(1, d, key))

    r64, c64 = iota((64, 64), 0), iota((64, 64), 1)
    e_row, e_lane = iota((64, 128), 0), iota((64, 128), 1)
    slot_of_row = 2 * (z * NY + (y + e_row // 16) % NY) + e_row % 2
    pick = jnp.where(e_lane == slot_of_row, 1.0, 0.0)
    block_of_row = ((r64 // 4) % 2) * 4 + ((r64 // 2) % 2) * 2 + (r64 // 8) % 2
    same_block = c64 // 8 == block_of_row
    scaled_row = (iota((64, 1), 0) // 8) % 2 == 1

    def select(i):
        ga, gb = gbuf[i, 0], gbuf[i, 1]
        tokens = jnp.concatenate(
            [ga[:8], ga[:8], ga[8:], ga[8:], gb[:8], gb[:8], gb[8:], gb[8:]], axis=0
        )
        table = nt(pick, tokens, precision=lax.Precision.HIGHEST)
        table = jnp.where(same_block, table, 0.0)
        scale = jnp.where(scaled_row, jnp.sum(table, axis=1, keepdims=True), 1.0)
        chosen = jnp.where(table > 0.0, 1.0, 0.0).astype(BF16)
        for n in range(0, D, TN):
            x = zbuf[i, :, :, pl.ds(n, TN)].reshape(64, TN)
            picked = jnp.dot(chosen, x, preferred_element_type=F32) * scale
            picked = picked.astype(BF16)
            ybuf[0, i, 0, :, pl.ds(n, TN)] = picked[:16]
            ysend[i, :, :, pl.ds(n, TN)] = picked[16:].reshape(NY - 1, 16, TN)
        for r in range(1, NY):
            send(
                ysend.at[i, r - 1], ybuf.at[0, i, NY - r],
                y_ss.at[i, r - 1], y_rs.at[i, r - 1], y_to[r],
            )

    def pass_on(i):
        for r in range(1, NY):
            arrived(ybuf.at[0, i, NY - r], y_rs.at[i, r - 1], y_to[r])
        send(ybuf.at[0, i], ybuf.at[1, i], f_ss.at[i], f_rs.at[i], partner)

    def part_rows(q, lane_of):
        g, qq = q // QG, q % QG
        for r in range(NY):
            for n in range(0, D, TN):
                two = ybuf[lane_of, pl.ds(2 * q, 2), r, :, pl.ds(n, TN)].astype(F32)
                at = pl.ds(r * 16, 16)
                rows_tok[g, lane_of, qq, at, pl.ds(n, TN)] = jnp.concatenate(
                    [two[0, :8], two[1, :8]], axis=0
                ).astype(BF16)
                rows_sc[g, lane_of, qq, at, pl.ds(n, TN)] = jnp.concatenate(
                    [two[0, 8:], two[1, 8:]], axis=0
                ).astype(BF16)

    def expert(g):
        rows = 2 * QG * 64
        tok = rows_tok[g].reshape(rows, D)
        sc = rows_sc[g].reshape(rows, D)
        pre = jnp.dot(tok, gu[...], preferred_element_type=F32)
        pre_gate, pre_up = pre[:, :H], pre[:, H:]
        sig = jax.nn.sigmoid(pre_gate)
        activated = pre_gate * sig
        hidden = activated * pre_up
        hidden_grad = nt(sc, down[...])
        gate_grad = hidden_grad * pre_up * sig * (1.0 + pre_gate * (1.0 - sig))
        both = jnp.concatenate(
            [gate_grad.astype(BF16), (hidden_grad * activated).astype(BF16)], axis=1
        )
        for n in range(0, D, TN):
            part = nt(both, gu[pl.ds(n, TN), :]).astype(BF16)
            part = part.reshape(2, QG, 64, TN)
            part_own[g, :, :, pl.ds(n, TN)] = part[0]
            part_send[g, :, :, pl.ds(n, TN)] = part[1]
        for qq in range(QG):
            send(
                part_send.at[g, qq], part_recv.at[g, qq],
                p_ss.at[g, qq], p_rs.at[g, qq], partner,
            )
        turned = hidden.T.astype(BF16)
        for n in range(0, D, TN):
            at = pl.ds(n, TN)
            sc_n = rows_sc[g, :, :, :, at].reshape(rows, TN)
            grad = jnp.dot(turned, sc_n, preferred_element_type=F32)
            cur_ref[:, at] = grad if g == 0 else cur_ref[:, at] + grad

    def give_back(q):
        g, qq = q // QG, q % QG
        arrived(part_recv.at[g, qq], p_rs.at[g, qq], partner)
        for n in range(0, D, TN):
            at = pl.ds(n, TN)
            total = part_own[g, qq, :, at].astype(F32) + part_recv[g, qq, :, at].astype(F32)
            total = total.astype(BF16)
            ebuf[q, 0, :, at] = total[:16]
            esend[q, :, :, at] = total[16:].reshape(NY - 1, 16, TN)
        for r in range(1, NY):
            send(
                esend.at[q, r - 1], ebuf.at[q, NY - r],
                e_ss.at[q, r - 1], e_rs.at[q, r - 1], y_to[r],
            )

    def combine(q):
        for r in range(1, NY):
            arrived(ebuf.at[q, NY - r], e_rs.at[q, r - 1], y_to[r])
        tokens = gbuf[pl.ds(2 * q, 2)].reshape(64, 128)
        table = nt(tokens, pick, precision=lax.Precision.HIGHEST)
        mine = (r64 // 8 == (c64 // 2) % 8) & (table > 0.0)
        chosen = jnp.where(mine, 1.0, 0.0).astype(BF16)
        for n in range(0, D, TN):
            x = ebuf[q, :, :, pl.ds(n, TN)].reshape(64, TN)
            total = jnp.dot(chosen, x, preferred_element_type=F32)
            cbuf[pl.ds(2 * q, 2), :, :, pl.ds(n, TN)] = total.reshape(2, 2, 16, TN)

    def ring(s, d, c):
        at = pl.ds(c * D2, D2)
        ss, rs = r_ss.at[d, s - 1, c], r_rs.at[d, s - 1, c]
        return rsend.at[d, s - 1, :, at], rrecv.at[d, s - 1, :, at], ss, rs, z_to[d]

    def sum_z():
        for c in range(2):
            rsend[c, 0, :, pl.ds(c * D2, D2)] = cbuf[K - 1, 1, :, pl.ds(c * D2, D2)].astype(BF16)
            send(*ring(1, c, c))
        yield
        for s in range(2, K + 1):
            for c in range(2):
                for d in range(2):
                    at = pl.ds(c * D2, D2)
                    total = cbuf[K - s, 1 - d, :, at]
                    if s > 2 or c == d:
                        _, dst, _, rs, dev = ring(s - 1, d, c)
                        arrived(dst, rs, dev)
                        total = total + rrecv[d, s - 2, :, at].astype(F32)
                    rsend[d, s - 1, :, at] = total.astype(BF16)
                    send(*ring(s, d, c))
            yield
        for c in range(2):
            at = pl.ds(c * D2, D2)
            total = cbuf[K - 1, 0, :, at]
            for d in range(2):
                _, dst, _, rs, dev = ring(K, d, c)
                arrived(dst, rs, dev)
                total = total + rrecv[d, K - 1, :, at].astype(F32)
            cot_ref[:, at] = total
        yield

    def newton():
        squares = jnp.zeros((8, 128), F32)
        for n in range(0, D, 128):
            piece = cur_ref[:, pl.ds(n, 128)]
            squares = squares + jnp.sum((piece * piece).reshape(H // 8, 8, 128), axis=0)
        nsend[...] = jnp.broadcast_to(jnp.sum(squares, keepdims=True), (8, 128))
        send(nsend, nrecv, n_ss, n_rs, partner)
        arrived(nrecv, n_rs, partner)
        yield
        norm = jnp.sqrt(nsend[...] + nrecv[...]) + 1e-07
        factor = (1.0 / norm)[:1, :1]
        for it in range(ITERS):
            mine = whole.at[it, me]
            for n in range(0, D, TN):
                at = pl.ds(n, TN)
                if it == 0:
                    value = cur_ref[:, at] * factor
                    cur_ref[:, at] = value
                    mine[:, at] = value.astype(BF16)
            send(mine, mine, x_ss.at[it], x_rs.at[it], partner)
            yield
            other = whole.at[it, 1 - me]
            gram_own = nt(mine[...], mine[...])
            yield
            arrived(other, x_rs.at[it], partner)
            gram_other = nt(mine[...], other[...])
            gm = gram_b.at[it, me]
            own_at = pl.ds(pl.multiple_of(me * H, H), H)
            other_at = pl.ds(pl.multiple_of((1 - me) * H, H), H)
            gm[:, own_at] = gram_own.astype(BF16)
            gm[:, other_at] = gram_other.astype(BF16)
            send(gm, gm, m_ss.at[it], m_rs.at[it], partner)
            yield
            arrived(gram_b.at[it, 1 - me], m_rs.at[it], partner)
            full = gram_b[it].reshape(2 * H, 2 * H)
            square = jnp.dot(gm[...], full, preferred_element_type=F32)
            sq_own = jnp.where(me == 0, square[:, :H], square[:, H:])
            sq_other = jnp.where(me == 0, square[:, H:], square[:, :H])
            p_own = (CUBIC * gram_own + QUINTIC * sq_own).astype(BF16)
            p_other = (CUBIC * gram_other + QUINTIC * sq_other).astype(BF16)
            yield
            for n in range(0, D, TN):
                at = pl.ds(n, TN)
                step = jnp.dot(p_own, mine[:, at], preferred_element_type=F32)
                step = step + jnp.dot(p_other, other[:, at], preferred_element_type=F32)
                value = LINEAR * cur_ref[:, at] + step
                cur_ref[:, at] = value
                if it + 1 < ITERS:
                    whole.at[it + 1, me][:, at] = value.astype(BF16)
            yield

    for s in range(1, K + 1):
        for d, key in pieces:
            if goes(s, d, key):
                arrived(*hop(s, d, key)[1::2], z_to[d])
                if goes(s + 1, d, key):
                    send(*hop(s + 1, d, key))
        select(s - 1)
        if s > 1:
            pass_on(s - 2)
        if s > 2:
            arrived(ybuf.at[1, s - 3], f_rs.at[s - 3], partner)
            if s % 2 == 0:
                for lane_of in range(2):
                    part_rows(s // 2 - 2, lane_of)
        if s == 1:
            for w in weights:
                w.wait()
    arrived(ybuf.at[1, K - 2], f_rs.at[K - 2], partner)
    pass_on(K - 1)
    for g in range(NG - 1):
        expert(g)
        for qq in range(QG):
            give_back(g * QG + qq)
    arrived(ybuf.at[1, K - 1], f_rs.at[K - 1], partner)
    for lane_of in range(2):
        part_rows(Q - 1, lane_of)
    expert(NG - 1)
    for qq in reversed(range(QG)):
        give_back((NG - 1) * QG + qq)
    for q in reversed(range(Q)):
        combine(q)
    run_both(sum_z(), newton())
    for c in pending:
        c.wait_send()


def on_device(activations, upstream, routes, route_gates, gate_matrix, up_matrix, down_matrix):
    NZ = lax.axis_size("expert") // NY
    K = NZ // 2
    Q = K // 2
    D = activations.shape[2]
    H = down_matrix.shape[1]
    QG = max(1, Q // 2)
    NG = Q // QG
    dma = pltpu.SemaphoreType.DMA
    vmem = pl.BlockSpec(memory_space=pltpu.VMEM)
    anywhere = pl.BlockSpec(memory_space=pl.ANY)
    cot, cur = pl.pallas_call(
        functools.partial(kernel, NZ),
        out_shape=(
            jax.ShapeDtypeStruct((16, D), F32),
            jax.ShapeDtypeStruct((H, D), F32),
        ),
        in_specs=[vmem] * 4 + [anywhere] * 3,
        out_specs=(vmem, vmem),
        scratch_shapes=[
            pltpu.VMEM((K, 2, 32, D), BF16),
            pltpu.VMEM((K, 2, 16, 128), F32),
            pltpu.VMEM((K, NY - 1, 16, D), BF16),
            pltpu.VMEM((2, K, NY, 16, D), BF16),
            pltpu.VMEM((NG, 2, QG, 64, D), BF16),
            pltpu.VMEM((NG, 2, QG, 64, D), BF16),
            pltpu.VMEM((D, 2 * H), BF16),
            pltpu.VMEM((H, D), BF16),
            pltpu.VMEM((NG, QG, 64, D), BF16),
            pltpu.VMEM((NG, QG, 64, D), BF16),
            pltpu.VMEM((NG, QG, 64, D), BF16),
            pltpu.VMEM((Q, NY - 1, 16, D), BF16),
            pltpu.VMEM((Q, NY, 16, D), BF16),
            pltpu.VMEM((K, 2, 16, D), F32),
            pltpu.VMEM((2, K, 16, D), BF16),
            pltpu.VMEM((2, K, 16, D), BF16),
            pltpu.VMEM((8, 128), F32),
            pltpu.VMEM((8, 128), F32),
            pltpu.VMEM((ITERS, 2, H, D), BF16),
            pltpu.VMEM((ITERS, 2, H, 2 * H), BF16),
            dma((3,)),
            dma((2, K, 2)), dma((2, K, 2)),
            dma((2, K)), dma((2, K)),
            dma((K, NY - 1)), dma((K, NY - 1)),
            dma((K,)), dma((K,)),
            dma((NG, QG)), dma((NG, QG)),
            dma((Q, NY - 1)), dma((Q, NY - 1)),
            dma((2, K, 2)), dma((2, K, 2)),
            dma(()), dma(()),
            dma((ITERS,)), dma((ITERS,)),
            dma((ITERS,)), dma((ITERS,)),
        ],
        compiler_params=pltpu.CompilerParams(collective_id=0, has_side_effects=True),
    )(activations, upstream, routes, route_gates, gate_matrix, up_matrix, down_matrix)
    update = (cur * math.sqrt(max(2 * H, D))).astype(BF16)
    return (cot.astype(BF16).reshape(2, 8, D), update[None])


def solution(mesh):
    rows = P(None, ("dp", "expert", "half"), None)
    return jax.shard_map(
        on_device,
        mesh=mesh,
        in_specs=(
            rows, rows, rows, rows,
            P("expert", None, "half"), P("expert", None, "half"), P("expert", "half", None),
        ),
        out_specs=(rows, P(("dp", "expert"), "half", None)),
        check_vma=False,
    )
```

time: 427 us -> 109 us (0.26)
  waiting for transfers between devices: 253 us -> 0 us
  Pallas kernels: 0 us -> 104 us
  starting transfers between devices: 71.8 us -> 0 us
  matrix products: 33.2 us -> 0 us
  local copies, waits for them, and re-layouts: 32.7 us -> 0 us
  between operations: 15.1 us -> 0.64 us
  blocking collectives: 10.4 us -> 0 us
  other arithmetic: 9.36 us -> 4.3 us
    all_to_all x6 -> x0, waiting for transfers between devices: 253 us -> none  [the longest x2 93.4 us: on_device(): lax.all_to_all(doubled_tokens, ('expert', 'half'), split_axis=0, concat_a...]
    pallas_call x0 -> x1, Pallas kernels: none -> 104 us  [on_device(): pl.pallas_call(functools.partial(kernel, NZ), out_shape=(jax.ShapeDtypeSt...]
    all_to_all x6 -> x0, starting transfers between devices: 71.7 us -> none  [the longest x2 30.7 us: on_device(): lax.all_to_all(doubled_tokens, ('expert', 'half'), split_axis=0, concat_a...]
    dot_general x22 -> x0, matrix products: 33.2 us -> none  [the longest x8 11.9 us: contract_last(): lax.dot_general(left, right, (((1,), (1,)), ((), ())), preferred_element_...]
    broadcast_in_dim x8 -> x0, local copies, waits for them, and re-layouts: 14.4 us -> none  [the longest x4 7.21 us: on_device(): jnp.broadcast_to(scaled_send[:, None], (experts, halves, capacity, width))]
    all_gather x2 -> x0, blocking collectives: 6.66 us -> none  [on_device(): lax.all_gather(gram_rows.astype(jnp.bfloat16), 'half', axis=0, tiled=True)]
    reshape x6 -> x0, local copies, waits for them, and re-layouts: 5.87 us -> none  [the longest x2 3.81 us: on_device(): rows_scaled = got_scaled.reshape(experts * halves * capacity, width)]
    reduce_sum x6 -> x0, other arithmetic: 4.81 us -> none  [the longest x2 4.31 us: on_device(): jnp.sum(returned.reshape(experts, halves, capacity, width).astype(jnp.flo...]
  transfers between devices with their start and end apart: 8 -> 0, of which waited for: 6 -> 0; matrix products, arithmetic and copies ran while one was open for 12% -> 0% of each run, Pallas kernels for 0% -> 0%
where the time goes in v1:
time: 109 us
  Pallas kernels  104 us (95%)
  other arithmetic  4.3 us (4%)
    pallas_call x1, Pallas kernels, on_device(): pl.pallas_call(functools.partial(kernel, NZ), out_shape=(jax.ShapeDtypeSt...  104 us
    broadcast_in_dim x1, other arithmetic, on_device(): return (cot.astype(BF16).reshape(2, 8, D), update[None])  2.76 us

profile of v1, /device:TPU:1, one launch (start us, length us, event | category | flops | bytes accessed | tf_op | source)
XLA Modules:
  0.0 108.8 jit_solution(3302886522870124482)
XLA Ops:
  0.6 103.9 %shard_map.86 = (f32[16,2048]{1,0:T(8,128)}, f32[256,2048]{1,0:T(8,128)}) custom-call(bf16[2,8,2048]{2,1,0:T(8,128)(2,1)} %act_ref.1, bf16[2,8,2048]{2,1,0:T(8,128)(2,1)} %ups_ref.1, s32[2,8,10]{2,1,0:T(8,128)} %routes_ref.1, f32[2,8,10]{2,1,0:T(8,128)} %gates_ref.1, bf16[1,2048,256]{2,1,0:T(8,128)(2,1)} %gate_hbm.1, bf16[1,2048,256]{2,1,0:T(8,128)(2,1)} %up_hbm.1, ...), custom_call_target="tpu_custom_call" | custom-call | tf_op jit(solution)/shard_map/pallas_call | solution.py:368
  104.5 1.5 %convert_bitcast_fusion = bf16[2,8,2048]{2,1,0:T(8,128)(2,1)} fusion(f32[16,2048]{1,0:T(8,128)} %get-tuple-element.4), kind=kLoop, calls=%fused_computation.2 | loop fusion | flops 32768 | bytes 196608 | tf_op jit(solution)/shard_map/reshape | solution.py:412
  106.1 2.8 %fusion = bf16[1,256,2048]{2,1,0:T(8,128)(2,1)} fusion(f32[256,2048]{1,0:T(8,128)} %get-tuple-element.5), kind=kLoop, calls=%fused_computation.1 | loop fusion | flops 1048576 | bytes 3145728 | tf_op jit(solution)/shard_map/broadcast_in_dim | solution.py:412

commit v2 on v1

--- a/solution.py
+++ b/solution.py
@@ -25,23 +25,19 @@
     return lax.broadcasted_iota(jnp.int32, shape, axis)
 
 
-def run_both(first, second):
-    live = [first, second]
-    while live:
-        for gen in list(live):
-            try:
-                next(gen)
-            except StopIteration:
-                live.remove(gen)
+def advance(gen, steps):
+    for _ in range(steps):
+        next(gen, None)
 
 
 def kernel(
-    NZ, act_ref, ups_ref, routes_ref, gates_ref, gate_hbm, up_hbm, down_hbm,
-    cot_ref, cur_ref,
+    NZ, act_hbm, ups_hbm, routes_hbm, gates_hbm, gate_hbm, up_hbm, down_hbm,
+    cot_hbm, upd_hbm,
+    act_ref, ups_ref, routes_ref, gates_ref, cot_ref, upd_ref, cur_ref, hid_t,
     zbuf, gbuf, ysend, ybuf, rows_tok, rows_sc, gu, down,
     part_own, part_send, part_recv, esend, ebuf, cbuf, rsend, rrecv,
     nsend, nrecv, whole, gram_b,
-    w_sem, z_ss, z_rs, g_ss, g_rs, y_ss, y_rs, f_ss, f_rs, p_ss, p_rs, e_ss, e_rs,
+    w_sem, o_sem, z_ss, z_rs, g_ss, g_rs, y_ss, y_rs, f_ss, f_rs, p_ss, p_rs, e_ss, e_rs,
     r_ss, r_rs, n_ss, n_rs, x_ss, x_rs, m_ss, m_rs,
 ):
     K = NZ // 2
@@ -50,8 +46,6 @@
     H = down.shape[0]
     D2 = D // 2
     TN = min(512, D)
-    QG = rows_tok.shape[2]
-    NG = Q // QG
     ex = lax.axis_index("expert")
     me = lax.axis_index("half")
     z = ex // NY
@@ -59,6 +53,7 @@
     z_up = {"expert": ((z + 1) % NZ) * NY + y}
     z_dn = {"expert": ((z + NZ - 1) % NZ) * NY + y}
     z_to = (z_up, z_dn)
+    z_two = tuple({"expert": ((z + NZ + h) % NZ) * NY + y} for h in (2, -2))
     y_to = [None] + [{"expert": z * NY + (y + r) % NY} for r in range(1, NY)]
     partner = {"half": 1 - me}
     pending = []
@@ -77,18 +72,29 @@
             device_id=dev, device_id_type=MESH,
         ).wait_recv()
 
-    weights = [
-        pltpu.make_async_copy(gate_hbm.at[0], gu.at[:, pl.ds(0, H)], w_sem.at[0]),
-        pltpu.make_async_copy(up_hbm.at[0], gu.at[:, pl.ds(H, H)], w_sem.at[1]),
-        pltpu.make_async_copy(down_hbm.at[0], down, w_sem.at[2]),
-    ]
-    for w in weights:
-        w.start()
-
     barrier = pltpu.get_barrier_semaphore()
-    peers = [z_up, z_dn, partner] + y_to[1:]
+    peers = [z_up, z_dn, *z_two, partner] + y_to[1:]
     for p in peers:
         pl.semaphore_signal(barrier, inc=1, device_id=p, device_id_type=MESH)
+
+    loads = [
+        pltpu.make_async_copy(src, dst, w_sem.at[n])
+        for n, (src, dst) in enumerate(
+            [
+                (routes_hbm, routes_ref),
+                (gates_hbm, gates_ref),
+                (act_hbm, act_ref),
+                (ups_hbm, ups_ref),
+                (gate_hbm.at[0], gu.at[:, pl.ds(0, H)]),
+                (up_hbm.at[0], gu.at[:, pl.ds(H, H)]),
+                (down_hbm.at[0], down),
+            ]
+        )
+    ]
+    for c in loads:
+        c.start()
+    for c in loads[:4]:
+        c.wait()
 
     lane = iota((8, 128), 1)
     sub = iota((8, 128), 0)
@@ -119,14 +125,16 @@
         dst = buf.at[s - 1, d] if s < K else buf.at[K - 1, 1]
         if key == "g":
             return src, dst, g_ss.at[d, s - 1], g_rs.at[d, s - 1], z_to[d]
-        rows = pl.ds(key * 16, 16)
-        ss, rs = z_ss.at[d, s - 1, key], z_rs.at[d, s - 1, key]
-        return src.at[rows], dst.at[rows], ss, rs, z_to[d]
+        m, c = key
+        at = (pl.ds(m * 16, 16), pl.ds(c * D2, D2))
+        ss, rs = z_ss.at[d, s - 1, 2 * m + c], z_rs.at[d, s - 1, 2 * m + c]
+        return src.at[at], dst.at[at], ss, rs, z_to[d]
 
     def goes(s, d, key):
-        return s < K or (s == K and (d == 0 if key == "g" else key == d))
-
-    pieces = [(d, key) for key in ("g", 0, 1) for d in range(2)]
+        return s < K or (s == K and (d == 0 if key == "g" else key[0] == d))
+
+    halves = [(m, c) for m in range(2) for c in range(2)]
+    pieces = [(d, key) for key in halves + ["g"] for d in range(2)]
     for d, key in pieces:
         send(*hop(1, d, key))
 
@@ -164,23 +172,23 @@
             arrived(ybuf.at[0, i, NY - r], y_rs.at[i, r - 1], y_to[r])
         send(ybuf.at[0, i], ybuf.at[1, i], f_ss.at[i], f_rs.at[i], partner)
 
-    def part_rows(q, lane_of):
-        g, qq = q // QG, q % QG
-        for r in range(NY):
-            for n in range(0, D, TN):
-                two = ybuf[lane_of, pl.ds(2 * q, 2), r, :, pl.ds(n, TN)].astype(F32)
-                at = pl.ds(r * 16, 16)
-                rows_tok[g, lane_of, qq, at, pl.ds(n, TN)] = jnp.concatenate(
-                    [two[0, :8], two[1, :8]], axis=0
-                ).astype(BF16)
-                rows_sc[g, lane_of, qq, at, pl.ds(n, TN)] = jnp.concatenate(
-                    [two[0, 8:], two[1, 8:]], axis=0
-                ).astype(BF16)
-
-    def expert(g):
-        rows = 2 * QG * 64
-        tok = rows_tok[g].reshape(rows, D)
-        sc = rows_sc[g].reshape(rows, D)
+    def part_rows(q):
+        for lane_of in range(2):
+            for r in range(NY):
+                for n in range(0, D, TN):
+                    two = ybuf[lane_of, pl.ds(2 * q, 2), r, :, pl.ds(n, TN)].astype(F32)
+                    at = pl.ds(r * 16, 16)
+                    rows_tok[q, lane_of, at, pl.ds(n, TN)] = jnp.concatenate(
+                        [two[0, :8], two[1, :8]], axis=0
+                    ).astype(BF16)
+                    rows_sc[q, lane_of, at, pl.ds(n, TN)] = jnp.concatenate(
+                        [two[0, 8:], two[1, 8:]], axis=0
+                    ).astype(BF16)
+
+    def expert(q, nq):
+        rows = nq * 128
+        tok = rows_tok[pl.ds(q, nq)].reshape(rows, D)
+        sc = rows_sc[pl.ds(q, nq)].reshape(rows, D)
         pre = jnp.dot(tok, gu[...], preferred_element_type=F32)
         pre_gate, pre_up = pre[:, :H], pre[:, H:]
         sig = jax.nn.sigmoid(pre_gate)
@@ -193,27 +201,24 @@
         )
         for n in range(0, D, TN):
             part = nt(both, gu[pl.ds(n, TN), :]).astype(BF16)
-            part = part.reshape(2, QG, 64, TN)
-            part_own[g, :, :, pl.ds(n, TN)] = part[0]
-            part_send[g, :, :, pl.ds(n, TN)] = part[1]
-        for qq in range(QG):
-            send(
-                part_send.at[g, qq], part_recv.at[g, qq],
-                p_ss.at[g, qq], p_rs.at[g, qq], partner,
-            )
-        turned = hidden.T.astype(BF16)
+            part = part.reshape(nq, 2, 64, TN)
+            part_own[pl.ds(q, nq), :, pl.ds(n, TN)] = part[:, 0]
+            part_send[pl.ds(q, nq), :, pl.ds(n, TN)] = part[:, 1]
+        for p in range(q, q + nq):
+            send(part_send.at[p], part_recv.at[p], p_ss.at[p], p_rs.at[p], partner)
+        hid_t[:, pl.ds(q * 128, rows)] = hidden.T.astype(BF16)
+
+    def down_grad():
         for n in range(0, D, TN):
             at = pl.ds(n, TN)
-            sc_n = rows_sc[g, :, :, :, at].reshape(rows, TN)
-            grad = jnp.dot(turned, sc_n, preferred_element_type=F32)
-            cur_ref[:, at] = grad if g == 0 else cur_ref[:, at] + grad
+            sc_n = rows_sc[:, :, :, at].reshape(Q * 128, TN)
+            cur_ref[:, at] = jnp.dot(hid_t[...], sc_n, preferred_element_type=F32)
 
     def give_back(q):
-        g, qq = q // QG, q % QG
-        arrived(part_recv.at[g, qq], p_rs.at[g, qq], partner)
+        arrived(part_recv.at[q], p_rs.at[q], partner)
         for n in range(0, D, TN):
             at = pl.ds(n, TN)
-            total = part_own[g, qq, :, at].astype(F32) + part_recv[g, qq, :, at].astype(F32)
+            total = part_own[q, :, at].astype(F32) + part_recv[q, :, at].astype(F32)
             total = total.astype(BF16)
             ebuf[q, 0, :, at] = total[:16]
             esend[q, :, :, at] = total[16:].reshape(NY - 1, 16, TN)
@@ -235,36 +240,43 @@
             total = jnp.dot(chosen, x, preferred_element_type=F32)
             cbuf[pl.ds(2 * q, 2), :, :, pl.ds(n, TN)] = total.reshape(2, 2, 16, TN)
 
-    def ring(s, d, c):
+    def chain(s, d, o, c):
         at = pl.ds(c * D2, D2)
-        ss, rs = r_ss.at[d, s - 1, c], r_rs.at[d, s - 1, c]
-        return rsend.at[d, s - 1, :, at], rrecv.at[d, s - 1, :, at], ss, rs, z_to[d]
+        sem = (d, o, s - 1, c)
+        dev = z_to[d] if o == 1 and s == Q else z_two[d]
+        buf = (d, o, s - 1, slice(None), at)
+        return rsend.at[buf], rrecv.at[buf], r_ss.at[sem], r_rs.at[sem], dev
+
+    def joins(s, d, o, c):
+        return s > 1 or o == 1 or c == d
 
     def sum_z():
-        for c in range(2):
-            rsend[c, 0, :, pl.ds(c * D2, D2)] = cbuf[K - 1, 1, :, pl.ds(c * D2, D2)].astype(BF16)
-            send(*ring(1, c, c))
-        yield
-        for s in range(2, K + 1):
-            for c in range(2):
-                for d in range(2):
-                    at = pl.ds(c * D2, D2)
-                    total = cbuf[K - s, 1 - d, :, at]
-                    if s > 2 or c == d:
-                        _, dst, _, rs, dev = ring(s - 1, d, c)
-                        arrived(dst, rs, dev)
-                        total = total + rrecv[d, s - 2, :, at].astype(F32)
-                    rsend[d, s - 1, :, at] = total.astype(BF16)
-                    send(*ring(s, d, c))
+        for s in range(1, Q + 1):
+            for o in range(2):
+                for c in range(2):
+                    for d in range(2):
+                        if not joins(s, d, o, c):
+                            continue
+                        at = pl.ds(c * D2, D2)
+                        k = K + 2 - 2 * s - o
+                        total = cbuf[k - 1, 1 if k == K else 1 - d, :, at]
+                        if s > 1 and joins(s - 1, d, o, c):
+                            _, dst, _, rs, dev = chain(s - 1, d, o, c)
+                            arrived(dst, rs, dev)
+                            total = total + rrecv[d, o, s - 2, :, at].astype(F32)
+                        rsend[d, o, s - 1, :, at] = total.astype(BF16)
+                        send(*chain(s, d, o, c))
             yield
         for c in range(2):
             at = pl.ds(c * D2, D2)
             total = cbuf[K - 1, 0, :, at]
-            for d in range(2):
-                _, dst, _, rs, dev = ring(K, d, c)
-                arrived(dst, rs, dev)
-                total = total + rrecv[d, K - 1, :, at].astype(F32)
-            cot_ref[:, at] = total
+            for o in range(2):
+                for d in range(2):
+                    if joins(Q, d, o, c):
+                        _, dst, _, rs, dev = chain(Q, d, o, c)
+                        arrived(dst, rs, dev)
+                        total = total + rrecv[d, o, Q - 1, :, at].astype(F32)
+            cot_ref[:, :, at] = total.reshape(2, 8, D2).astype(BF16)
         yield
 
     def newton():
@@ -313,10 +325,16 @@
                 step = jnp.dot(p_own, mine[:, at], preferred_element_type=F32)
                 step = step + jnp.dot(p_other, other[:, at], preferred_element_type=F32)
                 value = LINEAR * cur_ref[:, at] + step
-                cur_ref[:, at] = value
                 if it + 1 < ITERS:
+                    cur_ref[:, at] = value
                     whole.at[it + 1, me][:, at] = value.astype(BF16)
+                else:
+                    upd_ref[:, at] = (value * math.sqrt(max(2 * H, D))).astype(BF16)
             yield
+        pltpu.make_async_copy(upd_ref, upd_hbm, o_sem.at[0]).start()
+
+    def passed(i):
+        arrived(ybuf.at[1, i], f_rs.at[i], partner)
 
     for s in range(1, K + 1):
         for d, key in pieces:
@@ -325,33 +343,69 @@
                 if goes(s + 1, d, key):
                     send(*hop(s + 1, d, key))
         select(s - 1)
-        if s > 1:
-            pass_on(s - 2)
         if s > 2:
-            arrived(ybuf.at[1, s - 3], f_rs.at[s - 3], partner)
-            if s % 2 == 0:
-                for lane_of in range(2):
-                    part_rows(s // 2 - 2, lane_of)
-        if s == 1:
-            for w in weights:
-                w.wait()
-    arrived(ybuf.at[1, K - 2], f_rs.at[K - 2], partner)
+            pass_on(s - 3)
+        if s > 4 and s % 2 == 1:
+            passed(s - 5)
+            passed(s - 4)
+            part_rows((s - 5) // 2)
+    for w in loads[4:]:
+        w.wait()
+    for i in range(max(0, K - 2), K - 1):
+        pass_on(i)
+    if Q > 2:
+        passed(K - 4)
+        passed(K - 3)
+        first = Q - 2
+        for q in range(max(0, (K - 1 - 5) // 2 + 1), first + 1):
+            if q < first:
+                passed(2 * q)
+                passed(2 * q + 1)
+            part_rows(q)
+        expert(0, first)
     pass_on(K - 1)
-    for g in range(NG - 1):
-        expert(g)
-        for qq in range(QG):
-            give_back(g * QG + qq)
-    arrived(ybuf.at[1, K - 1], f_rs.at[K - 1], partner)
-    for lane_of in range(2):
-        part_rows(Q - 1, lane_of)
-    expert(NG - 1)
-    for qq in reversed(range(QG)):
-        give_back((NG - 1) * QG + qq)
-    for q in reversed(range(Q)):
+    if Q > 2:
+        for q in range(first):
+            give_back(q)
+    if Q > 1:
+        if Q == 2:
+            passed(0)
+            passed(1)
+            part_rows(0)
+        expert(Q - 2, 1)
+    passed(K - 2)
+    passed(K - 1)
+    part_rows(Q - 1)
+    expert(Q - 1, 1)
+    down_grad()
+    ns = newton()
+    give_back(Q - 1)
+    if Q > 1:
+        give_back(Q - 2)
+    for q in range(Q - 2):
         combine(q)
-    run_both(sum_z(), newton())
+    advance(ns, 2)
+    combine(Q - 1)
+    ring = sum_z()
+    advance(ring, 1)
+    if Q > 1:
+        combine(Q - 2)
+    for s in range(2, Q + 1):
+        advance(ns, 3)
+        advance(ring, 1)
+    advance(ns, 20)
+    advance(ring, 2)
+    cot_out = pltpu.make_async_copy(cot_ref, cot_hbm, o_sem.at[1])
+    cot_out.start()
     for c in pending:
         c.wait_send()
+    cot_out.wait()
+    pltpu.make_async_copy(upd_ref, upd_hbm, o_sem.at[0]).wait()
+
+
+def hand_over(cot_ref, upd_ref, cot_out, upd_out):
+    cot_out[...] = cot_ref[...]
+    upd_out[...] = upd_ref[...]
 
 
 def on_device(activations, upstream, routes, route_gates, gate_matrix, up_matrix, down_matrix):
@@ -360,56 +414,77 @@
     Q = K // 2
     D = activations.shape[2]
     H = down_matrix.shape[1]
-    QG = max(1, Q // 2)
-    NG = Q // QG
     dma = pltpu.SemaphoreType.DMA
-    vmem = pl.BlockSpec(memory_space=pltpu.VMEM)
     anywhere = pl.BlockSpec(memory_space=pl.ANY)
-    cot, cur = pl.pallas_call(
+    args = (activations, upstream, routes, route_gates, gate_matrix, up_matrix, down_matrix)
+    cot, upd = pl.pallas_call(
         functools.partial(kernel, NZ),
         out_shape=(
-            jax.ShapeDtypeStruct((16, D), F32),
-            jax.ShapeDtypeStruct((H, D), F32),
+            jax.ShapeDtypeStruct((2, 8, D), BF16),
+            jax.ShapeDtypeStruct((H, D), BF16),
         ),
-        in_specs=[vmem] * 4 + [anywhere] * 3,
-        out_specs=(vmem, vmem),
+        in_specs=[anywhere] * 7,
+        out_specs=(anywhere, anywhere),
         scratch_shapes=[
+            pltpu.VMEM(activations.shape, BF16),
+            pltpu.VMEM(upstream.shape, BF16),
+            pltpu.VMEM(routes.shape, routes.dtype),
+            pltpu.VMEM(route_gates.shape, F32),
+            pltpu.VMEM((2, 8, D), BF16),
+            pltpu.VMEM((H, D), BF16),
+            pltpu.VMEM((H, D), F32),
+            pltpu.VMEM((H, Q * 128), BF16),
             pltpu.VMEM((K, 2, 32, D), BF16),
             pltpu.VMEM((K, 2, 16, 128), F32),
             pltpu.VMEM((K, NY - 1, 16, D), BF16),
             pltpu.VMEM((2, K, NY, 16, D), BF16),
-            pltpu.VMEM((NG, 2, QG, 64, D), BF16),
-            pltpu.VMEM((NG, 2, QG, 64, D), BF16),
+            pltpu.VMEM((Q, 2, 64, D), BF16),
+            pltpu.VMEM((Q, 2, 64, D), BF16),
             pltpu.VMEM((D, 2 * H), BF16),
             pltpu.VMEM((H, D), BF16),
-            pltpu.VMEM((NG, QG, 64, D), BF16),
-            pltpu.VMEM((NG, QG, 64, D), BF16),
-            pltpu.VMEM((NG, QG, 64, D), BF16),
+            pltpu.VMEM((Q, 64, D), BF16),
+            pltpu.VMEM((Q, 64, D), BF16),
+            pltpu.VMEM((Q, 64, D), BF16),
             pltpu.VMEM((Q, NY - 1, 16, D), BF16),
             pltpu.VMEM((Q, NY, 16, D), BF16),
             pltpu.VMEM((K, 2, 16, D), F32),
-            pltpu.VMEM((2, K, 16, D), BF16),
-            pltpu.VMEM((2, K, 16, D), BF16),
+            pltpu.VMEM((2, 2, Q, 16, D), BF16),
+            pltpu.VMEM((2, 2, Q, 16, D), BF16),
             pltpu.VMEM((8, 128), F32),
             pltpu.VMEM((8, 128), F32),
             pltpu.VMEM((ITERS, 2, H, D), BF16),
             pltpu.VMEM((ITERS, 2, H, 2 * H), BF16),
-            dma((3,)),
-            dma((2, K, 2)), dma((2, K, 2)),
+            dma((7,)), dma((2,)),
+            dma((2, K, 4)), dma((2, K, 4)),
             dma((2, K)), dma((2, K)),
             dma((K, NY - 1)), dma((K, NY - 1)),
             dma((K,)), dma((K,)),
-            dma((NG, QG)), dma((NG, QG)),
+            dma((Q,)), dma((Q,)),
             dma((Q, NY - 1)), dma((Q, NY - 1)),
-            dma((2, K, 2)), dma((2, K, 2)),
+            dma((2, 2, Q, 2)), dma((2, 2, Q, 2)),
             dma(()), dma(()),
             dma((ITERS,)), dma((ITERS,)),
             dma((ITERS,)), dma((ITERS,)),
         ],
         compiler_params=pltpu.CompilerParams(collective_id=0, has_side_effects=True),
-    )(activations, upstream, routes, route_gates, gate_matrix, up_matrix, down_matrix)
-    update = (cur * math.sqrt(max(2 * H, D))).astype(BF16)
-    return (cot.astype(BF16).reshape(2, 8, D), update[None])
+    )(*args)
+    rows = H // 2
+    return pl.pallas_call(
+        hand_over,
+        out_shape=(
+            jax.ShapeDtypeStruct((2, 8, D), BF16),
+            jax.ShapeDtypeStruct((1, H, D), BF16),
+        ),
+        grid=(2,),
+        in_specs=[
+            pl.BlockSpec((2, 8, D), lambda i: (0, 0, 0)),
+            pl.BlockSpec((1, rows, D), lambda i: (0, i, 0)),
+        ],
+        out_specs=(
+            pl.BlockSpec((2, 8, D), lambda i: (0, 0, 0)),
+            pl.BlockSpec((1, rows, D), lambda i: (0, i, 0)),
+        ),
+    )(cot, upd[None])
 
 
 def solution(mesh):

time: 109 us -> 90.8 us (0.83)
  Pallas kernels: 104 us -> 90 us
  other arithmetic: 4.3 us -> 0 us
    pallas_call x1, Pallas kernels: 104 us -> 87.9 us  [on_device(): pl.pallas_call(functools.partial(kernel, NZ), out_shape=(jax.ShapeDtypeSt...]
    broadcast_in_dim x1 -> x0, other arithmetic: 2.76 us -> none  [on_device(): return (cot.astype(BF16).reshape(2, 8, D), update[None])]
    pallas_call x0 -> x1, Pallas kernels: none -> 2.09 us  [on_device(): pl.pallas_call(hand_over, out_shape=(jax.ShapeDtypeStruct((2, 8, D), BF16...]
    reshape x1 -> x0, other arithmetic: 1.54 us -> none  [on_device(): return (cot.astype(BF16).reshape(2, 8, D), update[None])]
where the time goes in v2:
time: 90.8 us; the launch traced here: 90.6 us
  Pallas kernels  90 us (99%)
    pallas_call x1, Pallas kernels, on_device(): pl.pallas_call(functools.partial(kernel, NZ), out_shape=(jax.ShapeDtypeSt...  87.9 us
    pallas_call x1, Pallas kernels, on_device(): pl.pallas_call(hand_over, out_shape=(jax.ShapeDtypeStruct((2, 8, D), BF16...  2.09 us

profile of v2, /device:TPU:1, one launch (start us, length us, event | category | flops | bytes accessed | tf_op | source)
XLA Modules:
  0.0 90.6 jit_solution(3222793128901859227)
XLA Ops:
  0.6 87.9 %shard_map.86 = (bf16[2,8,2048]{2,1,0:T(8,128)(2,1)}, bf16[256,2048]{1,0:T(8,128)(2,1)}) custom-call(bf16[2,8,2048]{2,1,0:T(8,128)(2,1)} %act_hbm.1, bf16[2,8,2048]{2,1,0:T(8,128)(2,1)} %ups_hbm.1, s32[2,8,10]{2,1,0:T(8,128)} %routes_hbm.1, f32[2,8,10]{2,1,0:T(8,128)} %gates_hbm.1, bf16[1,2048,256]{2,1,0:T(8,128)(2,1)} %gate_hbm.1, ...), custom_call_target="tpu_custom_call" | custom-call | tf_op jit(solution)/shard_map/pallas_call | solution.py:420
  88.5 2.1 %shard_map.87 = (bf16[2,8,2048]{2,1,0:T(8,128)(2,1)}, bf16[1,256,2048]{2,1,0:T(8,128)(2,1)}) custom-call(bf16[2,8,2048]{2,1,0:T(8,128)(2,1)} %get-tuple-element.4.cot_ref, bf16[1,256,2048]{2,1,0:T(8,128)(2,1)} %bitcast.1), custom_call_target="tpu_custom_call" | custom-call | tf_op jit(solution)/shard_map/pallas_call | solution.py:472

commit v3 on v2

--- a/solution.py
+++ b/solution.py
@@ -33,17 +33,17 @@
 def kernel(
     NZ, act_hbm, ups_hbm, routes_hbm, gates_hbm, gate_hbm, up_hbm, down_hbm,
     cot_hbm, upd_hbm,
-    act_ref, ups_ref, routes_ref, gates_ref, cot_ref, upd_ref, cur_ref, hid_t,
-    zbuf, gbuf, ysend, ybuf, rows_tok, rows_sc, gu, down,
-    part_own, part_send, part_recv, esend, ebuf, cbuf, rsend, rrecv,
+    act_ref, ups_ref, routes_ref, gates_ref, cot_ref, upd_ref, cur_ref, hid_own, hid_send, hid_in,
+    zbuf, gbuf, ysend, ybuf, rows_tok, rows_sc, rows_in, gu, down,
+    esend, ebuf, cbuf, rsend, rrecv,
     nsend, nrecv, whole, gram_b,
-    w_sem, o_sem, z_ss, z_rs, g_ss, g_rs, y_ss, y_rs, f_ss, f_rs, p_ss, p_rs, e_ss, e_rs,
+    w_sem, o_sem, z_ss, z_rs, g_ss, g_rs, y_ss, y_rs, f_ss, f_rs, p_ss, p_rs, v_ss, v_rs, e_ss, e_rs,
     r_ss, r_rs, n_ss, n_rs, x_ss, x_rs, m_ss, m_rs,
 ):
     K = NZ // 2
     Q = K // 2
     D = zbuf.shape[-1]
-    H = down.shape[0]
+    H = hid_own.shape[-1]
     D2 = D // 2
     TN = min(512, D)
     ex = lax.axis_index("expert")
@@ -87,7 +87,7 @@
                 (ups_hbm, ups_ref),
                 (gate_hbm.at[0], gu.at[:, pl.ds(0, H)]),
                 (up_hbm.at[0], gu.at[:, pl.ds(H, H)]),
-                (down_hbm.at[0], down),
+                (down_hbm.at[0], down.at[pl.ds(0, H)]),
             ]
         )
     ]
@@ -159,73 +159,79 @@
             x = zbuf[i, :, :, pl.ds(n, TN)].reshape(64, TN)
             picked = jnp.dot(chosen, x, preferred_element_type=F32) * scale
             picked = picked.astype(BF16)
-            ybuf[0, i, 0, :, pl.ds(n, TN)] = picked[:16]
+            ybuf[i, 0, :, pl.ds(n, TN)] = picked[:16]
             ysend[i, :, :, pl.ds(n, TN)] = picked[16:].reshape(NY - 1, 16, TN)
         for r in range(1, NY):
             send(
-                ysend.at[i, r - 1], ybuf.at[0, i, NY - r],
+                ysend.at[i, r - 1], ybuf.at[i, NY - r],
                 y_ss.at[i, r - 1], y_rs.at[i, r - 1], y_to[r],
             )
 
-    def pass_on(i):
-        for r in range(1, NY):
-            arrived(ybuf.at[0, i, NY - r], y_rs.at[i, r - 1], y_to[r])
-        send(ybuf.at[0, i], ybuf.at[1, i], f_ss.at[i], f_rs.at[i], partner)
-
     def part_rows(q):
-        for lane_of in range(2):
-            for r in range(NY):
-                for n in range(0, D, TN):
-                    two = ybuf[lane_of, pl.ds(2 * q, 2), r, :, pl.ds(n, TN)].astype(F32)
-                    at = pl.ds(r * 16, 16)
-                    rows_tok[q, lane_of, at, pl.ds(n, TN)] = jnp.concatenate(
-                        [two[0, :8], two[1, :8]], axis=0
-                    ).astype(BF16)
-                    rows_sc[q, lane_of, at, pl.ds(n, TN)] = jnp.concatenate(
-                        [two[0, 8:], two[1, 8:]], axis=0
-                    ).astype(BF16)
-
-    def expert(q, nq):
-        rows = nq * 128
-        tok = rows_tok[pl.ds(q, nq)].reshape(rows, D)
-        sc = rows_sc[pl.ds(q, nq)].reshape(rows, D)
-        pre = jnp.dot(tok, gu[...], preferred_element_type=F32)
-        pre_gate, pre_up = pre[:, :H], pre[:, H:]
-        sig = jax.nn.sigmoid(pre_gate)
-        activated = pre_gate * sig
-        hidden = activated * pre_up
-        hidden_grad = nt(sc, down[...])
-        gate_grad = hidden_grad * pre_up * sig * (1.0 + pre_gate * (1.0 - sig))
-        both = jnp.concatenate(
-            [gate_grad.astype(BF16), (hidden_grad * activated).astype(BF16)], axis=1
-        )
-        for n in range(0, D, TN):
-            part = nt(both, gu[pl.ds(n, TN), :]).astype(BF16)
-            part = part.reshape(nq, 2, 64, TN)
-            part_own[pl.ds(q, nq), :, pl.ds(n, TN)] = part[:, 0]
-            part_send[pl.ds(q, nq), :, pl.ds(n, TN)] = part[:, 1]
-        for p in range(q, q + nq):
-            send(part_send.at[p], part_recv.at[p], p_ss.at[p], p_rs.at[p], partner)
-        hid_t[:, pl.ds(q * 128, rows)] = hidden.T.astype(BF16)
-
-    def down_grad():
+        for i in (2 * q, 2 * q + 1):
+            for r in range(1, NY):
+                arrived(ybuf.at[i, NY - r], y_rs.at[i, r - 1], y_to[r])
+        for r in range(NY):
+            for n in range(0, D, TN):
+                two = ybuf[pl.ds(2 * q, 2), r, :, pl.ds(n, TN)].astype(F32)
+                at = pl.ds(r * 16, 16)
+                rows_tok[q, at, pl.ds(n, TN)] = jnp.concatenate(
+                    [two[0, :8], two[1, :8]], axis=0
+                ).astype(BF16)
+                rows_sc[q, at, pl.ds(n, TN)] = jnp.concatenate(
+                    [two[0, 8:], two[1, 8:]], axis=0
+                ).astype(BF16)
+        send(rows_sc.at[q], rows_in.at[q], f_ss.at[q], f_rs.at[q], partner)
+
+    def expert(q):
+        tok, sc = rows_tok[q], rows_sc[q]
+        boths = []
+        for j in range(2):
+            pre = jnp.dot(tok, gu[:, pl.ds(2 * H * j, 2 * H)], preferred_element_type=F32)
+            pre_gate, pre_up = pre[:, :H], pre[:, H:]
+            sig = jax.nn.sigmoid(pre_gate)
+            activated = pre_gate * sig
+            hidden = (activated * pre_up).astype(BF16)
+            hidden_grad = nt(sc, down[pl.ds(H * j, H), :])
+            gate_grad = hidden_grad * pre_up * sig * (1.0 + pre_gate * (1.0 - sig))
+            boths.append(
+                jnp.concatenate(
+                    [gate_grad.astype(BF16), (hidden_grad * activated).astype(BF16)], axis=1
+                )
+            )
+            if j == 0:
+                hid_own[q] = hidden
+            else:
+                hid_send[q] = hidden
         for n in range(0, D, TN):
             at = pl.ds(n, TN)
-            sc_n = rows_sc[:, :, :, at].reshape(Q * 128, TN)
-            cur_ref[:, at] = jnp.dot(hid_t[...], sc_n, preferred_element_type=F32)
-
-    def give_back(q):
-        arrived(part_recv.at[q], p_rs.at[q], partner)
-        for n in range(0, D, TN):
-            at = pl.ds(n, TN)
-            total = part_own[q, :, at].astype(F32) + part_recv[q, :, at].astype(F32)
-            total = total.astype(BF16)
+            parts = [
+                nt(boths[j], gu[at, pl.ds(2 * H * j, 2 * H)]).astype(BF16).astype(F32)
+                for j in range(2)
+            ]
+            total = (parts[0] + parts[1]).astype(BF16)
             ebuf[q, 0, :, at] = total[:16]
             esend[q, :, :, at] = total[16:].reshape(NY - 1, 16, TN)
         for r in range(1, NY):
             send(
                 esend.at[q, r - 1], ebuf.at[q, NY - r],
                 e_ss.at[q, r - 1], e_rs.at[q, r - 1], y_to[r],
+            )
+        send(hid_send.at[q], hid_in.at[q], p_ss.at[q], p_rs.at[q], partner)
+
+    def down_grad():
+        for q in range(Q):
+            arrived(rows_in.at[q], f_rs.at[q], partner)
+            arrived(hid_in.at[q], p_rs.at[q], partner)
+        own = hid_own[...].reshape(Q * 64, H).astype(F32).T.astype(BF16)
+        taken = hid_in[...].reshape(Q * 64, H).astype(F32).T.astype(BF16)
+        for n in range(0, D, TN):
+            at = pl.ds(n, TN)
+            grad = jnp.dot(
+                own, rows_sc[:, :, at].reshape(Q * 64, TN), preferred_element_type=F32
+            )
+            cur_ref[:, at] = grad + jnp.dot(
+                taken, rows_in[:, :, at].reshape(Q * 64, TN), preferred_element_type=F32
             )
 
     def combine(q):
@@ -240,42 +246,54 @@
             total = jnp.dot(chosen, x, preferred_element_type=F32)
             cbuf[pl.ds(2 * q, 2), :, :, pl.ds(n, TN)] = total.reshape(2, 2, 16, TN)
 
-    def chain(s, d, o, c):
+    def chain(s, d, c):
         at = pl.ds(c * D2, D2)
-        sem = (d, o, s - 1, c)
-        dev = z_to[d] if o == 1 and s == Q else z_two[d]
-        buf = (d, o, s - 1, slice(None), at)
-        return rsend.at[buf], rrecv.at[buf], r_ss.at[sem], r_rs.at[sem], dev
-
-    def joins(s, d, o, c):
-        return s > 1 or o == 1 or c == d
+        sem = (d, 0, s - 1, c)
+        buf = (d, 0, s - 1, slice(None), at)
+        return rsend.at[buf], rrecv.at[buf], r_ss.at[sem], r_rs.at[sem], z_two[d]
+
+    def side(s, d):
+        buf, sem = (d, 1, s - 1), (d, 1, s - 1, 0)
+        return rsend.at[buf], rrecv.at[buf], r_ss.at[sem], r_rs.at[sem], z_to[d]
+
+    def send_side(q):
+        for d in range(2):
+            rsend[d, 1, Q - q - 1] = cbuf[2 * q, 1 - d].astype(BF16)
+            send(*side(Q - q, d))
+
+    def got(copy):
+        arrived(copy[1], copy[3], copy[4])
 
     def sum_z():
         for s in range(1, Q + 1):
-            for o in range(2):
-                for c in range(2):
-                    for d in range(2):
-                        if not joins(s, d, o, c):
-                            continue
-                        at = pl.ds(c * D2, D2)
-                        k = K + 2 - 2 * s - o
-                        total = cbuf[k - 1, 1 if k == K else 1 - d, :, at]
-                        if s > 1 and joins(s - 1, d, o, c):
-                            _, dst, _, rs, dev = chain(s - 1, d, o, c)
-                            arrived(dst, rs, dev)
-                            total = total + rrecv[d, o, s - 2, :, at].astype(F32)
-                        rsend[d, o, s - 1, :, at] = total.astype(BF16)
-                        send(*chain(s, d, o, c))
+            for d in range(2):
+                if s > 1:
+                    got(side(s - 1, d))
+            for c in range(2):
+                for d in range(2):
+                    if s == 1 and c != d:
+                        continue
+                    at = pl.ds(c * D2, D2)
+                    k = K + 2 - 2 * s
+                    total = cbuf[k - 1, 1 if k == K else 1 - d, :, at]
+                    if s > 1:
+                        total = total + rrecv[d, 1, s - 2, :, at].astype(F32)
+                    if s > 2 or (s == 2 and c == d):
+                        got(chain(s - 1, d, c))
+                        total = total + rrecv[d, 0, s - 2, :, at].astype(F32)
+                    rsend[d, 0, s - 1, :, at] = total.astype(BF16)
+                    send(*chain(s, d, c))
             yield
+        for d in range(2):
+            got(side(Q, d))
         for c in range(2):
             at = pl.ds(c * D2, D2)
             total = cbuf[K - 1, 0, :, at]
-            for o in range(2):
-                for d in range(2):
-                    if joins(Q, d, o, c):
-                        _, dst, _, rs, dev = chain(Q, d, o, c)
-                        arrived(dst, rs, dev)
-                        total = total + rrecv[d, o, Q - 1, :, at].astype(F32)
+            for d in range(2):
+                total = total + rrecv[d, 1, Q - 1, :, at].astype(F32)
+                if Q > 1 or c == d:
+                    got(chain(Q, d, c))
+                    total = total + rrecv[d, 0, Q - 1, :, at].astype(F32)
             cot_ref[:, :, at] = total.reshape(2, 8, D2).astype(BF16)
         yield
 
@@ -286,8 +304,8 @@
             squares = squares + jnp.sum((piece * piece).reshape(H // 8, 8, 128), axis=0)
         nsend[...] = jnp.broadcast_to(jnp.sum(squares, keepdims=True), (8, 128))
         send(nsend, nrecv, n_ss, n_rs, partner)
+        yield
         arrived(nrecv, n_rs, partner)
-        yield
         norm = jnp.sqrt(nsend[...] + nrecv[...]) + 1e-07
         factor = (1.0 / norm)[:1, :1]
         for it in range(ITERS):
@@ -333,9 +351,15 @@
             yield
         pltpu.make_async_copy(upd_ref, upd_hbm, o_sem.at[0]).start()
 
-    def passed(i):
-        arrived(ybuf.at[1, i], f_rs.at[i], partner)
-
+    shares = [
+        (gate_hbm.at[0], gu.at[:, pl.ds(2 * H, H)]),
+        (up_hbm.at[0], gu.at[:, pl.ds(3 * H, H)]),
+        (down_hbm.at[0], down.at[pl.ds(H, H)]),
+    ]
+    for n, (src, dst) in enumerate(shares):
+        send(src, dst, v_ss.at[n], v_rs.at[n], partner)
+
+    done = 0
     for s in range(1, K + 1):
         for d, key in pieces:
             if goes(s, d, key):
@@ -343,53 +367,31 @@
                 if goes(s + 1, d, key):
                     send(*hop(s + 1, d, key))
         select(s - 1)
-        if s > 2:
-            pass_on(s - 3)
-        if s > 4 and s % 2 == 1:
-            passed(s - 5)
-            passed(s - 4)
-            part_rows((s - 5) // 2)
-    for w in loads[4:]:
-        w.wait()
-    for i in range(max(0, K - 2), K - 1):
-        pass_on(i)
-    if Q > 2:
-        passed(K - 4)
-        passed(K - 3)
-        first = Q - 2
-        for q in range(max(0, (K - 1 - 5) // 2 + 1), first + 1):
-            if q < first:
-                passed(2 * q)
-                passed(2 * q + 1)
-            part_rows(q)
-        expert(0, first)
-    pass_on(K - 1)
-    if Q > 2:
-        for q in range(first):
-            give_back(q)
-    if Q > 1:
-        if Q == 2:
-            passed(0)
-            passed(1)
-            part_rows(0)
-        expert(Q - 2, 1)
-    passed(K - 2)
-    passed(K - 1)
-    part_rows(Q - 1)
-    expert(Q - 1, 1)
+        if s == K - 2 or (s == K and K < 3):
+            for c in loads[4:]:
+                c.wait()
+            for n, (_, dst) in enumerate(shares):
+                arrived(dst, v_rs.at[n], partner)
+        if s >= K - 2 and 2 * done + 3 < s:
+            part_rows(done)
+            expert(done)
+            done += 1
+    for q in range(done, Q):
+        part_rows(q)
+        expert(q)
+    for q in range(Q - 2):
+        combine(q)
+        send_side(q)
     down_grad()
     ns = newton()
-    give_back(Q - 1)
-    if Q > 1:
-        give_back(Q - 2)
-    for q in range(Q - 2):
-        combine(q)
-    advance(ns, 2)
+    advance(ns, 1)
     combine(Q - 1)
     ring = sum_z()
     advance(ring, 1)
+    send_side(Q - 1)
     if Q > 1:
         combine(Q - 2)
+        send_side(Q - 2)
     for s in range(2, Q + 1):
         advance(ns, 3)
         advance(ring, 1)
@@ -433,18 +435,18 @@
             pltpu.VMEM((2, 8, D), BF16),
             pltpu.VMEM((H, D), BF16),
             pltpu.VMEM((H, D), F32),
-            pltpu.VMEM((H, Q * 128), BF16),
+            pltpu.VMEM((Q, 64, H), BF16),
+            pltpu.VMEM((Q, 64, H), BF16),
+            pltpu.VMEM((Q, 64, H), BF16),
             pltpu.VMEM((K, 2, 32, D), BF16),
             pltpu.VMEM((K, 2, 16, 128), F32),
             pltpu.VMEM((K, NY - 1, 16, D), BF16),
-            pltpu.VMEM((2, K, NY, 16, D), BF16),
-            pltpu.VMEM((Q, 2, 64, D), BF16),
-            pltpu.VMEM((Q, 2, 64, D), BF16),
-            pltpu.VMEM((D, 2 * H), BF16),
-            pltpu.VMEM((H, D), BF16),
+            pltpu.VMEM((K, NY, 16, D), BF16),
             pltpu.VMEM((Q, 64, D), BF16),
             pltpu.VMEM((Q, 64, D), BF16),
             pltpu.VMEM((Q, 64, D), BF16),
+            pltpu.VMEM((D, 4 * H), BF16),
+            pltpu.VMEM((2 * H, D), BF16),
             pltpu.VMEM((Q, NY - 1, 16, D), BF16),
             pltpu.VMEM((Q, NY, 16, D), BF16),
             pltpu.VMEM((K, 2, 16, D), F32),
@@ -458,8 +460,9 @@
             dma((2, K, 4)), dma((2, K, 4)),
             dma((2, K)), dma((2, K)),
             dma((K, NY - 1)), dma((K, NY - 1)),
-            dma((K,)), dma((K,)),
             dma((Q,)), dma((Q,)),
+            dma((Q,)), dma((Q,)),
+            dma((3,)), dma((3,)),
             dma((Q, NY - 1)), dma((Q, NY - 1)),
             dma((2, 2, Q, 2)), dma((2, 2, Q, 2)),
             dma(()), dma(()),

time: 90.8 us -> 84.1 us (0.926)
  Pallas kernels: 90 us -> 82.7 us
    pallas_call x1, Pallas kernels: 87.9 us -> 80.7 us  [on_device(): pl.pallas_call(functools.partial(kernel, NZ), out_shape=(jax.ShapeDtypeSt...]
where the time goes in v3:
time: 84.1 us; the launch traced here: 83.4 us
  Pallas kernels  82.7 us (98%)
    pallas_call x1, Pallas kernels, on_device(): pl.pallas_call(functools.partial(kernel, NZ), out_shape=(jax.ShapeDtypeSt...  80.7 us
    pallas_call x1, Pallas kernels, on_device(): pl.pallas_call(hand_over, out_shape=(jax.ShapeDtypeStruct((2, 8, D), BF16...  2.09 us

profile of v3, /device:TPU:1, one launch (start us, length us, event | category | flops | bytes accessed | tf_op | source)
XLA Modules:
  0.0 83.4 jit_solution(14501775854924755524)
XLA Ops:
  0.6 80.7 %shard_map.86 = (bf16[2,8,2048]{2,1,0:T(8,128)(2,1)}, bf16[256,2048]{1,0:T(8,128)(2,1)}) custom-call(bf16[2,8,2048]{2,1,0:T(8,128)(2,1)} %act_hbm.1, bf16[2,8,2048]{2,1,0:T(8,128)(2,1)} %ups_hbm.1, s32[2,8,10]{2,1,0:T(8,128)} %routes_hbm.1, f32[2,8,10]{2,1,0:T(8,128)} %gates_hbm.1, bf16[1,2048,256]{2,1,0:T(8,128)(2,1)} %gate_hbm.1, ...), custom_call_target="tpu_custom_call" | custom-call | tf_op jit(solution)/shard_map/pallas_call | solution.py:422
  81.3 2.1 %shard_map.87 = (bf16[2,8,2048]{2,1,0:T(8,128)(2,1)}, bf16[1,256,2048]{2,1,0:T(8,128)(2,1)}) custom-call(bf16[2,8,2048]{2,1,0:T(8,128)(2,1)} %get-tuple-element.4.cot_ref, bf16[1,256,2048]{2,1,0:T(8,128)(2,1)} %bitcast.1), custom_call_target="tpu_custom_call" | custom-call | tf_op jit(solution)/shard_map/pallas_call | solution.py:475

commit v4 on v3

--- a/solution.py
+++ b/solution.py
@@ -33,7 +33,7 @@
 def kernel(
     NZ, act_hbm, ups_hbm, routes_hbm, gates_hbm, gate_hbm, up_hbm, down_hbm,
     cot_hbm, upd_hbm,
-    act_ref, ups_ref, routes_ref, gates_ref, cot_ref, upd_ref, cur_ref, hid_own, hid_send, hid_in,
+    act_ref, ups_ref, routes_ref, gates_ref, cot_ref, upd_ref, cur_ref, hid_own, hid_send, hid_in, both,
     zbuf, gbuf, ysend, ybuf, rows_tok, rows_sc, rows_in, gu, down,
     esend, ebuf, cbuf, rsend, rrecv,
     nsend, nrecv, whole, gram_b,
@@ -183,41 +183,43 @@
                 ).astype(BF16)
         send(rows_sc.at[q], rows_in.at[q], f_ss.at[q], f_rs.at[q], partner)
 
-    def expert(q):
-        tok, sc = rows_tok[q], rows_sc[q]
-        boths = []
+    def expert(q, nq):
+        rows = nq * 64
+        at_q = pl.ds(q, nq)
         for j in range(2):
+            tok = rows_tok[at_q].reshape(rows, D)
             pre = jnp.dot(tok, gu[:, pl.ds(2 * H * j, 2 * H)], preferred_element_type=F32)
             pre_gate, pre_up = pre[:, :H], pre[:, H:]
             sig = jax.nn.sigmoid(pre_gate)
             activated = pre_gate * sig
             hidden = (activated * pre_up).astype(BF16)
-            hidden_grad = nt(sc, down[pl.ds(H * j, H), :])
+            hidden_grad = nt(rows_sc[at_q].reshape(rows, D), down[pl.ds(H * j, H), :])
             gate_grad = hidden_grad * pre_up * sig * (1.0 + pre_gate * (1.0 - sig))
-            boths.append(
-                jnp.concatenate(
-                    [gate_grad.astype(BF16), (hidden_grad * activated).astype(BF16)], axis=1
-                )
-            )
+            both[j, pl.ds(0, rows), pl.ds(0, H)] = gate_grad.astype(BF16)
+            both[j, pl.ds(0, rows), pl.ds(H, H)] = (hidden_grad * activated).astype(BF16)
             if j == 0:
-                hid_own[q] = hidden
+                hid_own[at_q] = hidden.reshape(nq, 64, H)
             else:
-                hid_send[q] = hidden
+                hid_send[at_q] = hidden.reshape(nq, 64, H)
+            yield
         for n in range(0, D, TN):
             at = pl.ds(n, TN)
             parts = [
-                nt(boths[j], gu[at, pl.ds(2 * H * j, 2 * H)]).astype(BF16).astype(F32)
+                nt(both[j, pl.ds(0, rows)], gu[at, pl.ds(2 * H * j, 2 * H)])
                 for j in range(2)
             ]
-            total = (parts[0] + parts[1]).astype(BF16)
-            ebuf[q, 0, :, at] = total[:16]
-            esend[q, :, :, at] = total[16:].reshape(NY - 1, 16, TN)
-        for r in range(1, NY):
-            send(
-                esend.at[q, r - 1], ebuf.at[q, NY - r],
-                e_ss.at[q, r - 1], e_rs.at[q, r - 1], y_to[r],
-            )
-        send(hid_send.at[q], hid_in.at[q], p_ss.at[q], p_rs.at[q], partner)
+            parts = [p.astype(BF16).astype(F32) for p in parts]
+            total = (parts[0] + parts[1]).astype(BF16).reshape(nq, 64, TN)
+            ebuf[at_q, 0, :, at] = total[:, :16]
+            esend[at_q, :, :, at] = total[:, 16:].reshape(nq, NY - 1, 16, TN)
+        for p in range(q, q + nq):
+            for r in (2, 1, 3):
+                send(
+                    esend.at[p, r - 1], ebuf.at[p, NY - r],
+                    e_ss.at[p, r - 1], e_rs.at[p, r - 1], y_to[r],
+                )
+            send(hid_send.at[p], hid_in.at[p], p_ss.at[p], p_rs.at[p], partner)
+        yield
 
     def down_grad():
         for q in range(Q):
@@ -359,7 +361,14 @@
     for n, (src, dst) in enumerate(shares):
         send(src, dst, v_ss.at[n], v_rs.at[n], partner)
 
-    done = 0
+    def weights_here():
+        for c in loads[4:]:
+            c.wait()
+        for n, (_, dst) in enumerate(shares):
+            arrived(dst, v_rs.at[n], partner)
+
+    early = max(0, Q - 2)
+    first = iter(())
     for s in range(1, K + 1):
         for d, key in pieces:
             if goes(s, d, key):
@@ -367,18 +376,18 @@
                 if goes(s + 1, d, key):
                     send(*hop(s + 1, d, key))
         select(s - 1)
-        if s == K - 2 or (s == K and K < 3):
-            for c in loads[4:]:
-                c.wait()
-            for n, (_, dst) in enumerate(shares):
-                arrived(dst, v_rs.at[n], partner)
-        if s >= K - 2 and 2 * done + 3 < s:
-            part_rows(done)
-            expert(done)
-            done += 1
-    for q in range(done, Q):
+        if early and s == K - 2:
+            weights_here()
+            for q in range(early):
+                part_rows(q)
+            first = expert(0, early)
+        advance(first, 1)
+    advance(first, 3)
+    if not early:
+        weights_here()
+    for q in range(early, Q):
         part_rows(q)
-        expert(q)
+        advance(expert(q, 1), 3)
     for q in range(Q - 2):
         combine(q)
         send_side(q)
@@ -438,6 +447,7 @@
             pltpu.VMEM((Q, 64, H), BF16),
             pltpu.VMEM((Q, 64, H), BF16),
             pltpu.VMEM((Q, 64, H), BF16),
+            pltpu.VMEM((2, max(1, Q - 2) * 64, 2 * H), BF16),
             pltpu.VMEM((K, 2, 32, D), BF16),
             pltpu.VMEM((K, 2, 16, 128), F32),
             pltpu.VMEM((K, NY - 1, 16, D), BF16),

time: 84.1 us -> 81.8 us (0.973)
  Pallas kernels: 82.7 us -> 81 us
    pallas_call x1, Pallas kernels: 80.7 us -> 78.9 us  [on_device(): pl.pallas_call(functools.partial(kernel, NZ), out_shape=(jax.ShapeDtypeSt...]
where the time goes in v4:
time: 81.8 us; the launch traced here: 81.7 us
  Pallas kernels  81 us (99%)
    pallas_call x1, Pallas kernels, on_device(): pl.pallas_call(functools.partial(kernel, NZ), out_shape=(jax.ShapeDtypeSt...  78.9 us
    pallas_call x1, Pallas kernels, on_device(): pl.pallas_call(hand_over, out_shape=(jax.ShapeDtypeStruct((2, 8, D), BF16...  2.09 us

profile of v4, /device:TPU:1, one launch (start us, length us, event | category | flops | bytes accessed | tf_op | source)
XLA Modules:
  0.0 81.7 jit_solution(12251688359656253732)
XLA Ops:
  0.6 78.9 %shard_map.86 = (bf16[2,8,2048]{2,1,0:T(8,128)(2,1)}, bf16[256,2048]{1,0:T(8,128)(2,1)}) custom-call(bf16[2,8,2048]{2,1,0:T(8,128)(2,1)} %act_hbm.1, bf16[2,8,2048]{2,1,0:T(8,128)(2,1)} %ups_hbm.1, s32[2,8,10]{2,1,0:T(8,128)} %routes_hbm.1, f32[2,8,10]{2,1,0:T(8,128)} %gates_hbm.1, bf16[1,2048,256]{2,1,0:T(8,128)(2,1)} %gate_hbm.1, ...), custom_call_target="tpu_custom_call" | custom-call | tf_op jit(solution)/shard_map/pallas_call | solution.py:431
  79.6 2.1 %shard_map.87 = (bf16[2,8,2048]{2,1,0:T(8,128)(2,1)}, bf16[1,256,2048]{2,1,0:T(8,128)(2,1)}) custom-call(bf16[2,8,2048]{2,1,0:T(8,128)(2,1)} %get-tuple-element.4.cot_ref, bf16[1,256,2048]{2,1,0:T(8,128)(2,1)} %bitcast.1), custom_call_target="tpu_custom_call" | custom-call | tf_op jit(solution)/shard_map/pallas_call | solution.py:485

commit v5 on v4

--- a/solution.py
+++ b/solution.py
@@ -202,24 +202,29 @@
             else:
                 hid_send[at_q] = hidden.reshape(nq, 64, H)
             yield
-        for n in range(0, D, TN):
-            at = pl.ds(n, TN)
+        TW = min(TN, D2)
+        for n in range(0, D, TW):
+            at = pl.ds(n, TW)
             parts = [
                 nt(both[j, pl.ds(0, rows)], gu[at, pl.ds(2 * H * j, 2 * H)])
                 for j in range(2)
             ]
             parts = [p.astype(BF16).astype(F32) for p in parts]
-            total = (parts[0] + parts[1]).astype(BF16).reshape(nq, 64, TN)
+            total = (parts[0] + parts[1]).astype(BF16).reshape(nq, 64, TW)
             ebuf[at_q, 0, :, at] = total[:, :16]
-            esend[at_q, :, :, at] = total[:, 16:].reshape(nq, NY - 1, 16, TN)
+            esend[at_q, :, :, at] = total[:, 16:].reshape(nq, NY - 1, 16, TW)
+            if (n + TW) % D2 == 0:
+                for p in range(q, q + nq):
+                    for r in (2, 1, 3):
+                        send(*back(p, r, n // D2))
         for p in range(q, q + nq):
-            for r in (2, 1, 3):
-                send(
-                    esend.at[p, r - 1], ebuf.at[p, NY - r],
-                    e_ss.at[p, r - 1], e_rs.at[p, r - 1], y_to[r],
-                )
             send(hid_send.at[p], hid_in.at[p], p_ss.at[p], p_rs.at[p], partner)
         yield
+
+    def back(q, r, c):
+        at = pl.ds(c * D2, D2)
+        src, dst = esend.at[q, r - 1, :, at], ebuf.at[q, NY - r, :, at]
+        return src, dst, e_ss.at[q, r - 1, c], e_rs.at[q, r - 1, c], y_to[r]
 
     def down_grad():
         for q in range(Q):
@@ -238,7 +243,8 @@
 
     def combine(q):
         for r in range(1, NY):
-            arrived(ebuf.at[q, NY - r], e_rs.at[q, r - 1], y_to[r])
+            for c in range(2):
+                arrived(*back(q, r, c)[1::2], y_to[r])
         tokens = gbuf[pl.ds(2 * q, 2)].reshape(64, 128)
         table = nt(tokens, pick, precision=lax.Precision.HIGHEST)
         mine = (r64 // 8 == (c64 // 2) % 8) & (table > 0.0)
@@ -402,7 +408,7 @@
         combine(Q - 2)
         send_side(Q - 2)
     for s in range(2, Q + 1):
-        advance(ns, 3)
+        advance(ns, (2, 1, 4)[(s - 2) % 3])
         advance(ring, 1)
     advance(ns, 20)
     advance(ring, 2)
@@ -414,9 +420,21 @@
     pltpu.make_async_copy(upd_ref, upd_hbm, o_sem.at[0]).wait()
 
 
-def hand_over(cot_ref, upd_ref, cot_out, upd_out):
-    cot_out[...] = cot_ref[...]
-    upd_out[...] = upd_ref[...]
+def hand_over(cot_ref, upd_ref, cot_out, upd_out, cot_mem, upd_mem, in_sem, out_sem):
+    rows = upd_mem.shape[0] // 4
+    parts = [(cot_ref, cot_mem, cot_out)]
+    for n in range(4):
+        at = pl.ds(n * rows, rows)
+        parts.append((upd_ref.at[at], upd_mem.at[at], upd_out.at[0, at]))
+    into = [pltpu.make_async_copy(p[0], p[1], in_sem.at[n]) for n, p in enumerate(parts)]
+    out = [pltpu.make_async_copy(p[1], p[2], out_sem.at[n]) for n, p in enumerate(parts)]
+    for c in into:
+        c.start()
+    for c, o in zip(into, out):
+        c.wait()
+        o.start()
+    for o in out:
+        o.wait()
 
 
 def on_device(activations, upstream, routes, route_gates, gate_matrix, up_matrix, down_matrix):
@@ -473,7 +491,7 @@
             dma((Q,)), dma((Q,)),
             dma((Q,)), dma((Q,)),
             dma((3,)), dma((3,)),
-            dma((Q, NY - 1)), dma((Q, NY - 1)),
+            dma((Q, NY - 1, 2)), dma((Q, NY - 1, 2)),
             dma((2, 2, Q, 2)), dma((2, 2, Q, 2)),
             dma(()), dma(()),
             dma((ITERS,)), dma((ITERS,)),
@@ -481,23 +499,18 @@
         ],
         compiler_params=pltpu.CompilerParams(collective_id=0, has_side_effects=True),
     )(*args)
-    rows = H // 2
     return pl.pallas_call(
         hand_over,
         out_shape=(
             jax.ShapeDtypeStruct((2, 8, D), BF16),
             jax.ShapeDtypeStruct((1, H, D), BF16),
         ),
-        grid=(2,),
-        in_specs=[
-            pl.BlockSpec((2, 8, D), lambda i: (0, 0, 0)),
-            pl.BlockSpec((1, rows, D), lambda i: (0, i, 0)),
+        in_specs=[anywhere] * 2,
+        out_specs=(anywhere, anywhere),
+        scratch_shapes=[
+            pltpu.VMEM((2, 8, D), BF16), pltpu.VMEM((H, D), BF16), dma((5,)), dma((5,)),
         ],
-        out_specs=(
-            pl.BlockSpec((2, 8, D), lambda i: (0, 0, 0)),
-            pl.BlockSpec((1, rows, D), lambda i: (0, i, 0)),
-        ),
-    )(cot, upd[None])
+    )(cot, upd)
 
 
 def solution(mesh):

time: 81.8 us -> 82.3 us (level)
  no operation moved by 1% of the time
where the time goes in v5:
time: 82.3 us; the launch traced here: 82.2 us
  Pallas kernels  81.5 us (99%)
    pallas_call x1, Pallas kernels, on_device(): pl.pallas_call(functools.partial(kernel, NZ), out_shape=(jax.ShapeDtypeSt...  79.5 us
    pallas_call x1, Pallas kernels, on_device(): pl.pallas_call(hand_over, out_shape=(jax.ShapeDtypeStruct((2, 8, D), BF16...  2.04 us

profile of v5, /device:TPU:1, one launch (start us, length us, event | category | flops | bytes accessed | tf_op | source)
XLA Modules:
  0.0 82.2 jit_solution(17995778144297916240)
XLA Ops:
  0.6 79.5 %shard_map.86 = (bf16[2,8,2048]{2,1,0:T(8,128)(2,1)}, bf16[256,2048]{1,0:T(8,128)(2,1)}) custom-call(bf16[2,8,2048]{2,1,0:T(8,128)(2,1)} %act_hbm.1, bf16[2,8,2048]{2,1,0:T(8,128)(2,1)} %ups_hbm.1, s32[2,8,10]{2,1,0:T(8,128)} %routes_hbm.1, f32[2,8,10]{2,1,0:T(8,128)} %gates_hbm.1, bf16[1,2048,256]{2,1,0:T(8,128)(2,1)} %gate_hbm.1, ...), custom_call_target="tpu_custom_call" | custom-call | tf_op jit(solution)/shard_map/pallas_call | solution.py:449
  80.1 2.0 %shard_map.87 = (bf16[2,8,2048]{2,1,0:T(8,128)(2,1)}, bf16[1,256,2048]{2,1,0:T(8,128)(2,1)}) custom-call(bf16[2,8,2048]{2,1,0:T(8,128)(2,1)} %get-tuple-element.4.cot_ref, bf16[256,2048]{1,0:T(8,128)(2,1)} %get-tuple-element.5.upd_ref), custom_call_target="tpu_custom_call" | custom-call | tf_op jit(solution)/shard_map/pallas_call | solution.py:502
